TPU v7x, 32 devices: a whole 2x2x4 slice. The times are simulated.
32 devices in a mesh: img: 16 (over z, y, x), ref: 2 (over core).
Axes of the slice: x: 2, y: 2, z: 4, core: 2. Of those that a mesh axis runs over, the one named last changes fastest.
Arguments:
- images: bfloat16 [16384, 2048], P('img'), may hold values from -8 to 8
- references: bfloat16 [1024, 2048], P('ref'), may hold values from -1 to 1
- initial_contrast: float32 [16384], P('img'), may hold values from 0.25 to 1.75
Outputs:
- new_references: bfloat16 [1024, 2048], P('ref')
- contrast: float32 [16384], P('img')
- loglik: float32 [16384], P('img')
All inputs are finite; a program needn't handle non-finite values.
Results may differ from a plain program's by a relative error of at most 0.0041.
Values may be sent and summed in bfloat16 or wider, within the bound.
A program may use at most 64 MiB of HBM per device.

v0:
```python
import functools
import math

import jax
import jax.numpy as jnp
from jax import lax
from jax.experimental import pallas as pl
from jax.experimental.pallas import tpu as pltpu
from jax.sharding import PartitionSpec as P

ITERS = 3

sharpness = 2.0
prior_weight = 1.0
epsilon = 1e-06

MESH = pl.DeviceIdType.MESH
LANES = 256
QUADS = ((1, 0), (1, 1), (0, 1), (0, 0))
F32 = jnp.float32
BF16 = jnp.bfloat16


def kernel(
    nz, n_ref, im_hbm, ref_hbm, prior_ref, newref_hbm, contrast_ref, loglik_ref,
    im, refs, norms, cross, w, snd1, rcv1, acc, snd2, rcv2, snd3, rcv3, gath,
    stat_snd, stat_rcv, vecs, im_sem, ref_sem, out_sem, ssem, rsem,
):
    n, width = im.shape
    rows = refs.shape[0]
    rb = rows // (4 * nz)
    qr = nz * rb
    half = width // 2
    me = lax.axis_index("img")
    rme = lax.axis_index("ref")
    x, y, z = lax.rem(me, 2), lax.rem(me // 2, 2), me // 4
    counter = [0]

    def chip(dx, dy, dz):
        zz, bit = z, 1
        while bit < nz:
            if dz & bit:
                zz = zz + bit - 2 * bit * lax.rem(z // bit, 2)
            bit *= 2
        return zz * 4 + lax.rem(y + dy, 2) * 2 + lax.rem(x + dx, 2)

    def send(src, dst, dev):
        i = counter[0]
        counter[0] += 1
        copy = pltpu.make_async_remote_copy(
            src_ref=src, dst_ref=dst, send_sem=ssem.at[i], recv_sem=rsem.at[i],
            device_id=dev, device_id_type=MESH,
        )
        copy.start()
        sent.append(copy)
        return copy

    sent = []
    x_dev = {"img": chip(1, 0, 0)}
    y_dev = {"img": chip(0, 1, 0)}
    z_dev = [{"img": chip(0, 0, k)} for k in range(nz)]
    r_dev = [{"ref": lax.rem(rme + k, n_ref)} for k in range(n_ref)]

    ref_copies = []
    for q, (dx, dy) in enumerate(QUADS):
        for dz in range(nz):
            s = q * nz + dz
            copy = pltpu.make_async_copy(
                ref_hbm.at[pl.ds(chip(dx, dy, dz) * rb, rb)],
                refs.at[pl.ds(s * rb, rb)], ref_sem.at[s],
            )
            copy.start()
            ref_copies.append(copy)
    im_copies = []
    for b in range(n // LANES):
        part = pl.ds(b * LANES, LANES)
        copy = pltpu.make_async_copy(im_hbm.at[part], im.at[part], im_sem.at[b])
        copy.start()
        im_copies.append(copy)

    barrier = pltpu.get_barrier_semaphore()
    peers = [x_dev, y_dev] + [z_dev[k] for k in range(1, nz) if k & (k - 1) == 0] + r_dev[1:]
    for dev in peers:
        pl.semaphore_signal(barrier, inc=1, device_id=dev, device_id_type=MESH)

    stat_snd[...] = jnp.zeros_like(stat_snd)
    vecs[0:1, :] = prior_ref[...]

    def square_sums(source, r0, count, scale):
        block = source[r0 : r0 + count, :].astype(F32)
        total = jnp.sum(block * block, axis=1, keepdims=True) * scale
        norms[r0 : r0 + count, :] = jnp.broadcast_to(total, (count, LANES))

    for s, copy in enumerate(ref_copies):
        copy.wait()
        square_sums(refs, s * rb, rb, 1.0)

    nt = (((1,), (1,)), ((), ()))
    nn = (((1,), (0,)), ((), ()))
    for copy in im_copies:
        copy.wait()

    def score_block(source, r0, count, scale):
        def body(b, carry):
            part = pl.ds(pl.multiple_of(b * LANES, LANES), LANES)
            out = lax.dot_general(
                source[r0 : r0 + count, :], im[part, :], nt, preferred_element_type=F32
            )
            cross[r0 : r0 + count, part] = out if scale is None else out * scale
            return carry

        lax.fori_loop(0, n // LANES, body, 0)

    score_block(refs, 0, rows, None)
    pl.semaphore_wait(barrier, len(peers))

    def scored(part):
        a = vecs[0:1, part]
        c = cross[:, part]
        return c, (sharpness * a) * c - ((0.5 * sharpness) * (a * a)) * norms[...]

    def statistics(it, full):
        def body(b, carry):
            part = pl.ds(pl.multiple_of(b * LANES, LANES), LANES)
            c, s = scored(part)
            top = jnp.max(s, axis=0, keepdims=True)
            e = jnp.exp(s - top)
            stat_snd[it, 0:1, part] = top
            stat_snd[it, 1:2, part] = jnp.sum(e, axis=0, keepdims=True)
            if full:
                stat_snd[it, 2:3, part] = jnp.sum(e * c, axis=0, keepdims=True)
                stat_snd[it, 3:4, part] = jnp.sum(e * norms[...], axis=0, keepdims=True)
            return carry

        lax.fori_loop(0, n // LANES, body, 0)
        copies = [
            send(stat_snd.at[it], stat_rcv.at[it * (n_ref - 1) + k - 1], r_dev[k])
            for k in range(1, n_ref)
        ]
        for copy in copies:
            copy.wait_recv()
        blocks = [stat_snd[it]] + [
            stat_rcv[it * (n_ref - 1) + k - 1] for k in range(1, n_ref)
        ]
        high = functools.reduce(jnp.maximum, [blk[0:1] for blk in blocks])
        scales = [jnp.exp(blk[0:1] - high) for blk in blocks]
        sums = [
            functools.reduce(jnp.add, [blk[j : j + 1] * sc for blk, sc in zip(blocks, scales)])
            for j in ((1, 2, 3) if full else (1,))
        ]
        return high, sums

    for it in range(ITERS):
        high, (total, along, weight) = statistics(it, True)
        vecs[0:1, :] = (along / total + prior_weight * prior_ref[...]) / (
            weight / total + prior_weight
        )
    high, (total,) = statistics(ITERS, False)
    vecs[1:2, :] = high
    vecs[2:3, :] = vecs[0:1, :] / total
    contrast_ref[...] = vecs[0:1, :]

    def weigh(b, carry):
        part = pl.ds(pl.multiple_of(b * LANES, LANES), LANES)
        _, s = scored(part)
        w[:, part] = (jnp.exp(s - vecs[1:2, part]) * vecs[2:3, part]).astype(BF16)
        return carry

    lax.fori_loop(0, n // LANES, weigh, 0)

    def weighted(r0s, c0, store):
        def body(b, carry):
            col = pl.multiple_of(b * LANES, LANES)
            lhs = [w[r0 : r0 + cnt, :] for r0, cnt in r0s]
            lhs = lhs[0] if len(lhs) == 1 else jnp.concatenate(lhs, axis=0)
            rhs = im[:, pl.ds(pl.multiple_of(c0 + col, LANES), LANES)]
            out = lax.dot_general(lhs, rhs, nn, preferred_element_type=F32)
            store(pl.ds(col, LANES), out[:qr], out[qr:])
            return carry

        lax.fori_loop(0, half // LANES, body, 0)

    def to_send(stream, first_is_far):
        def store(cols, lo, hi):
            far, near = (lo, hi) if first_is_far else (hi, lo)
            snd1[stream * 2, :, cols] = far.astype(BF16)
            snd1[stream * 2 + 1, :, cols] = near.astype(BF16)

        return store

    def to_keep(stream):
        def store(cols, lo, hi):
            acc[stream * 2, :, cols] = lo
            acc[stream * 2 + 1, :, cols] = hi

        return store

    low = [dz & -dz for dz in range(nz)]
    order = sorted(range(1, nz), key=lambda k: (low[k], -k)) + [0]
    early = [dz for dz in order if low[dz] == 1] or order
    late = [dz for dz in order if dz not in early]
    hop_dev = (x_dev, y_dev)
    step1 = {}

    def send1(s, j, dzs):
        for dz in dzs:
            part = pl.ds(dz * rb, rb)
            step1[s, j, dz] = send(
                snd1.at[s * 2 + j, part], rcv1.at[s * 2 + j, part], hop_dev[s]
            )

    weighted([(0, 2 * qr)], 0, to_send(0, False))
    send1(0, 0, early)
    send1(0, 1, early)
    weighted([(qr, 2 * qr)], half, to_send(1, True))
    send1(1, 0, early)
    send1(1, 1, early)
    weighted([(2 * qr, 2 * qr)], 0, to_keep(0))
    weighted([(0, qr), (3 * qr, qr)], half, to_keep(1))

    step2 = {}

    def send2(dzs):
        for dz in dzs:
            r0 = dz * rb
            part = pl.ds(r0, rb)
            for s in (1, 0):
                step1[s, 0, dz].wait_recv()
                snd2[s, r0 : r0 + rb, :] = (
                    acc[s * 2, r0 : r0 + rb, :] + rcv1[s * 2, r0 : r0 + rb, :].astype(F32)
                ).astype(BF16)
                step2[s, dz] = send(snd2.at[s, part], rcv2.at[s, part], hop_dev[1 - s])

    def gained(s, dz):
        step1[s, 1, dz].wait_recv()
        step2[s, dz].wait_recv()
        r0 = dz * rb
        return (
            acc[s * 2 + 1, r0 : r0 + rb, :]
            + rcv1[s * 2 + 1, r0 : r0 + rb, :].astype(F32)
            + rcv2[s, r0 : r0 + rb, :].astype(F32)
        )

    step3 = {}

    def complete(s, dz):
        total = gained(s, dz)
        for k in range(nz):
            if low[k] and k - low[k] == dz and (dz == 0 or low[k] < low[dz]):
                step3[s, k].wait_recv()
                total = total + rcv3[s, k - 1].astype(F32)
        return total

    def send3(dzs):
        for dz in dzs:
            for s in (0, 1):
                snd3[s, dz - 1] = complete(s, dz).astype(BF16)
                step3[s, dz] = send(
                    snd3.at[s, dz - 1], rcv3.at[s, dz - 1], z_dev[low[dz]]
                )

    send2(early)
    middle = [dz for dz in late if dz]
    final = [dz for dz in late if not dz]
    for j, dzs in ((0, middle), (1, middle), (0, final)):
        for s in (0, 1):
            send1(s, j, dzs)
    if late:
        send3(early)
    send2(middle)
    for s in (0, 1):
        send1(s, 1, final)
    send2(final)
    send3(middle)
    for s in (0, 1):
        acc[s * 2 + 1, 0:rb, :] = complete(s, 0)

    left, right = acc[1, 0:rb, :], acc[3, 0:rb, :]
    square = jnp.sum(left * left, axis=1, keepdims=True) + jnp.sum(
        right * right, axis=1, keepdims=True
    )
    factor = lax.rsqrt(square / width + epsilon)
    own = 3 * qr
    gath[own : own + rb, 0:half] = (left * factor).astype(BF16)
    gath[own : own + rb, half:width] = (right * factor).astype(BF16)

    def piece(q, dz, s):
        return gath.at[pl.ds(q * qr + dz * rb, rb), pl.ds(s * half, half)]

    def slot(q, dz):
        return gath.at[pl.ds(q * qr + dz * rb, rb)]

    along_z = {}

    def double(dz, bits):
        for bit in bits:
            along_z[dz + bit] = send(slot(3, dz), slot(3, dz + bit), z_dev[bit])

    bits = [1 << j for j in range(nz.bit_length() - 1)]
    into_x, into_y, last = {}, {}, []

    def spread(dz):
        into_y[dz] = [send(piece(3, dz, 0), piece(2, dz, 0), y_dev)]
        into_x[dz] = [send(piece(3, dz, 1), piece(0, dz, 1), x_dev)]
        into_y[dz].append(send(piece(3, dz, 1), piece(2, dz, 1), y_dev))
        into_x[dz].append(send(piece(3, dz, 0), piece(0, dz, 0), x_dev))

    def forward(dz):
        into_y[dz][0].wait_recv()
        last.append(send(piece(2, dz, 0), piece(1, dz, 0), x_dev))
        into_x[dz][0].wait_recv()
        last.append(send(piece(0, dz, 1), piece(1, dz, 1), y_dev))

    outs = []

    def finish(q):
        dx, dy = QUADS[q]
        for dz in range(nz):
            copy = pltpu.make_async_copy(
                slot(q, dz), newref_hbm.at[pl.ds(chip(dx, dy, dz) * rb, rb)],
                out_sem.at[q * nz + dz],
            )
            copy.start()
            outs.append(copy)
        square_sums(gath, q * qr, qr, 1.0 / width)

    double(0, bits)
    spread(0)
    arrivals = sorted(range(1, nz), key=lambda k: (k.bit_count(), k))
    before = 0
    for dz in arrivals:
        along_z[dz].wait_recv()
        double(dz, [bit for bit in bits if bit < low[dz]])
        spread(dz)
        forward(before)
        before = dz
    forward(before)
    for dz in range(nz):
        into_y[dz][1].wait_recv()
    finish(3)
    finish(2)
    score_block(gath, 2 * qr, 2 * qr, width ** (-0.5))
    for dz in range(nz):
        into_x[dz][1].wait_recv()
    finish(0)
    for copy in last:
        copy.wait_recv()
    finish(1)
    score_block(gath, 0, 2 * qr, width ** (-0.5))

    high, (total,) = statistics(ITERS + 1, False)
    loglik_ref[...] = high + jnp.log(total) - math.log(rows * n_ref)
    for copy in outs:
        copy.wait()
    for copy in sent:
        copy.wait_send()


def per_device(nz, n_ref, images, references, initial_contrast):
    n, width = images.shape
    rows = references.shape[0]
    rb = rows // (4 * nz)
    qr, half = nz * rb, width // 2
    steps = ITERS + 2
    copies = steps * (n_ref - 1) + 6 * nz + 2 * (nz - 1) + (nz - 1) + 6 * nz
    peers = max(n_ref - 1, 1)
    flops = 6 * n * width * rows
    new_references, contrast, loglik = pl.pallas_call(
        functools.partial(kernel, nz, n_ref),
        out_shape=(
            pltpu.VMEM((rows, width), BF16),
            pltpu.VMEM((1, n), F32),
            pltpu.VMEM((1, n), F32),
        ),
        in_specs=[
            pl.BlockSpec(memory_space=pl.ANY),
            pl.BlockSpec(memory_space=pl.ANY),
            pl.BlockSpec(memory_space=pltpu.VMEM),
        ],
        out_specs=(
            pl.BlockSpec(memory_space=pltpu.VMEM),
            pl.BlockSpec(memory_space=pltpu.VMEM),
            pl.BlockSpec(memory_space=pltpu.VMEM),
        ),
        scratch_shapes=[
            pltpu.VMEM((n, width), BF16),
            pltpu.VMEM((rows, width), BF16),
            pltpu.VMEM((rows, LANES), F32),
            pltpu.VMEM((rows, n), F32),
            pltpu.VMEM((rows, n), BF16),
            pltpu.VMEM((4, qr, half), BF16),
            pltpu.VMEM((4, qr, half), BF16),
            pltpu.VMEM((4, qr, half), F32),
            pltpu.VMEM((2, qr, half), BF16),
            pltpu.VMEM((2, qr, half), BF16),
            pltpu.VMEM((2, max(nz - 1, 1), rb, half), BF16),
            pltpu.VMEM((2, max(nz - 1, 1), rb, half), BF16),
            pltpu.VMEM((rows, width), BF16),
            pltpu.VMEM((steps, 4, n), F32),
            pltpu.VMEM((steps * peers, 4, n), F32),
            pltpu.VMEM((8, n), F32),
            pltpu.SemaphoreType.DMA((n // LANES,)),
            pltpu.SemaphoreType.DMA((4 * nz,)),
            pltpu.SemaphoreType.DMA((4 * nz,)),
            pltpu.SemaphoreType.DMA((copies,)),
            pltpu.SemaphoreType.DMA((copies,)),
        ],
        compiler_params=pltpu.CompilerParams(
            collective_id=0, has_side_effects=True, vmem_limit_bytes=56 * 1024 * 1024
        ),
        cost_estimate=pl.CostEstimate(
            flops=flops, bytes_accessed=2 * n * width, transcendentals=0
        ),
    )(images, references, initial_contrast[None, :])
    return (new_references, contrast[0], loglik[0])


def solution(mesh):
    n_img, n_ref = mesh.shape["img"], mesh.shape["ref"]
    placed = (P("img", None), P("ref", None), P("img"))
    return jax.shard_map(
        functools.partial(per_device, n_img // 4, n_ref),
        mesh=mesh,
        in_specs=placed,
        out_specs=(P("ref", None), P("img"), P("img")),
        check_vma=False,
    )
```

profile of v0, /device:TPU:0, one launch (start us, length us, event | category | flops | bytes accessed | tf_op | source)
XLA Modules:
  0.0 75.5 jit_solution(11038105640280352735)
XLA Ops:
  0.6 72.4 %shard_map.58 = (bf16[512,2048]{1,0:T(8,128)(2,1)S(1)}, f32[1,1024]{1,0:T(1,128)S(1)}, f32[1,1024]{1,0:T(1,128)S(1)}) custom-call(bf16[1024,2048]{1,0:T(8,128)(2,1)} %im_hbm.1, bf16[512,2048]{1,0:T(8,128)(2,1)} %ref_hbm.1, f32[1,1024]{1,0:T(1,128)} %bitcast.5), custom_call_target="tpu_custom_call" | custom-call | flops 6442450944 | bytes 4194304 | tf_op jit(solution)/shard_map/pallas_call | solution.py:368
  73.0 1.3 %copy.9 = bf16[512,2048]{1,0:T(8,128)(2,1)} copy(bf16[512,2048]{1,0:T(8,128)(2,1)S(1)} %get-tuple-element.9) | data formatting | bytes 4194304
  74.3 0.6 copy.10
  74.9 0.6 copy.11
where the time goes:
time: 75.7 us; the launch traced here: 75.5 us
  Pallas kernels  72.4 us (96%)
  local copies, waits for them, and re-layouts  2.51 us (3%)
    pallas_call x1, Pallas kernels, per_device(): pl.pallas_call(functools.partial(kernel, nz, n_ref), out_shape=(pltpu.VME...  72.4 us
    unnamed x3, local copies, waits for them, and re-layouts  2.51 us

commit v1 on v0

--- a/solution.py
+++ b/solution.py
@@ -16,6 +16,9 @@
 
 MESH = pl.DeviceIdType.MESH
 LANES = 256
+BLOCK = 512
+ROWS = 64
+LOG2E = math.log2(math.e)
 QUADS = ((1, 0), (1, 1), (0, 1), (0, 0))
 F32 = jnp.float32
 BF16 = jnp.bfloat16
@@ -24,9 +27,12 @@
 def kernel(
     nz, n_ref, im_hbm, ref_hbm, prior_ref, newref_hbm, contrast_ref, loglik_ref,
     im, refs, norms, cross, w, snd1, rcv1, acc, snd2, rcv2, snd3, rcv3, gath,
-    stat_snd, stat_rcv, vecs, im_sem, ref_sem, out_sem, ssem, rsem,
+    stat_snd, stat_rcv, vecs, keep, *rest,
 ):
     n, width = im.shape
+    *split, im_sem, ref_sem, out_sem, ssem, rsem = rest
+    paired = bool(split)
+    mine = n // n_ref
     rows = refs.shape[0]
     rb = rows // (4 * nz)
     qr = nz * rb
@@ -73,10 +79,15 @@
             ref_copies.append(copy)
     im_copies = []
     for b in range(n // LANES):
+        at = b * LANES
+        if paired:
+            at = lax.rem(rme * mine + at, n)
         part = pl.ds(b * LANES, LANES)
-        copy = pltpu.make_async_copy(im_hbm.at[part], im.at[part], im_sem.at[b])
-        copy.start()
+        copy = pltpu.make_async_copy(im_hbm.at[pl.ds(at, LANES)], im.at[part], im_sem.at[b])
         im_copies.append(copy)
+    first_theirs = mine // LANES if paired else 0
+    for b in range(n // LANES):
+        im_copies[(b + first_theirs) % (n // LANES)].start()
 
     barrier = pltpu.get_barrier_semaphore()
     peers = [x_dev, y_dev] + [z_dev[k] for k in range(1, nz) if k & (k - 1) == 0] + r_dev[1:]
@@ -84,12 +95,21 @@
         pl.semaphore_signal(barrier, inc=1, device_id=dev, device_id_type=MESH)
 
     stat_snd[...] = jnp.zeros_like(stat_snd)
-    vecs[0:1, :] = prior_ref[...]
+
+    def lanes_of(k):
+        return pl.ds(pl.multiple_of(lax.rem(rme + k, n_ref) * mine, 128), mine)
+
+    if paired:
+        for k in range(n_ref):
+            vecs[0:1, k * mine : (k + 1) * mine] = prior_ref[:, lanes_of(k)]
+    else:
+        vecs[0:1, :] = prior_ref[...]
+    vecs[3:4, :] = vecs[0:1, :]
 
     def square_sums(source, r0, count, scale):
         block = source[r0 : r0 + count, :].astype(F32)
         total = jnp.sum(block * block, axis=1, keepdims=True) * scale
-        norms[r0 : r0 + count, :] = jnp.broadcast_to(total, (count, LANES))
+        norms[r0 : r0 + count, :] = jnp.broadcast_to(total, (count, 128))
 
     for s, copy in enumerate(ref_copies):
         copy.wait()
@@ -97,8 +117,6 @@
 
     nt = (((1,), (1,)), ((), ()))
     nn = (((1,), (0,)), ((), ()))
-    for copy in im_copies:
-        copy.wait()
 
     def score_block(source, r0, count, scale):
         def body(b, carry):
@@ -111,62 +129,193 @@
 
         lax.fori_loop(0, n // LANES, body, 0)
 
-    score_block(refs, 0, rows, None)
-    pl.semaphore_wait(barrier, len(peers))
-
-    def scored(part):
-        a = vecs[0:1, part]
-        c = cross[:, part]
-        return c, (sharpness * a) * c - ((0.5 * sharpness) * (a * a)) * norms[...]
+    def fold(x):
+        return x.reshape(x.shape[0] // 8, 8, 128)
+
+    def spread8(x):
+        return jnp.broadcast_to(x, (8, 128))
+
+    def coefficients(c0, width_):
+        a = vecs[0:1, c0 : c0 + width_]
+        slope = (sharpness * LOG2E) * a
+        bend = (0.5 * sharpness * LOG2E) * (a * a)
+        tiles = range(0, width_, 128)
+        return (
+            [spread8(slope[:, t : t + 128]) for t in tiles],
+            [spread8(bend[:, t : t + 128]) for t in tiles],
+        )
+
+    def over_rows(count, body, init):
+        return lax.fori_loop(
+            0, count // ROWS, lambda i, c: body(pl.multiple_of(i * ROWS, ROWS), c), init
+        )
+
+    def scores(parts, c0, width_, keep):
+        slope, bend = coefficients(c0, width_)
+        tiles = width_ // 128
+        high = tuple(jnp.full((8, 128), -jnp.inf, F32) for _ in range(tiles))
+        k0 = 0
+        for values, norm, v0 in parts:
+
+            def body(r, high, values=values, norm=norm, v0=v0, k0=k0):
+                rows_ = pl.ds(r, ROWS)
+                nrm = fold(norm[rows_, :])
+                out = []
+                for t in range(tiles):
+                    c = fold(values[rows_, v0 + t * 128 : v0 + (t + 1) * 128])
+                    sc = slope[t][None] * c - bend[t][None] * nrm
+                    keep[pl.ds(k0 + r, ROWS), t * 128 : (t + 1) * 128] = sc.reshape(ROWS, 128)
+                    out.append(jnp.maximum(high[t], jnp.max(sc, axis=0)))
+                return tuple(out)
+
+            high = over_rows(values.shape[0], body, high)
+            k0 += values.shape[0]
+        return [jnp.max(h, axis=0, keepdims=True) for h in high]
+
+    def sums_of(parts, high, keep, full):
+        tiles = len(high)
+        top = [spread8(h) for h in high]
+        zero = jnp.zeros((8, 128), F32)
+        carry = tuple(zero for _ in range(tiles * (3 if full else 1)))
+        k0 = 0
+        for values, norm, v0 in parts:
+
+            def body(r, carry, values=values, norm=norm, v0=v0, k0=k0):
+                rows_ = pl.ds(r, ROWS)
+                nrm = fold(norm[rows_, :]) if full else None
+                out = list(carry)
+                for t in range(tiles):
+                    sc = fold(keep[pl.ds(k0 + r, ROWS), t * 128 : (t + 1) * 128])
+                    e = jnp.exp2(sc - top[t][None])
+                    out[t] = out[t] + jnp.sum(e, axis=0)
+                    if full:
+                        c = fold(values[rows_, v0 + t * 128 : v0 + (t + 1) * 128])
+                        out[tiles + t] = out[tiles + t] + jnp.sum(e * c, axis=0)
+                        out[2 * tiles + t] = out[2 * tiles + t] + jnp.sum(e * nrm, axis=0)
+                return tuple(out)
+
+            carry = over_rows(values.shape[0], body, carry)
+            k0 += values.shape[0]
+        return [jnp.sum(x, axis=0, keepdims=True) for x in carry]
 
     def statistics(it, full):
-        def body(b, carry):
-            part = pl.ds(pl.multiple_of(b * LANES, LANES), LANES)
-            c, s = scored(part)
-            top = jnp.max(s, axis=0, keepdims=True)
-            e = jnp.exp(s - top)
-            stat_snd[it, 0:1, part] = top
-            stat_snd[it, 1:2, part] = jnp.sum(e, axis=0, keepdims=True)
-            if full:
-                stat_snd[it, 2:3, part] = jnp.sum(e * c, axis=0, keepdims=True)
-                stat_snd[it, 3:4, part] = jnp.sum(e * norms[...], axis=0, keepdims=True)
-            return carry
-
-        lax.fori_loop(0, n // LANES, body, 0)
+        for c0 in range(0, n, BLOCK):
+            parts = [(cross, norms, c0)]
+            high = scores(parts, c0, BLOCK, keep)
+            sums = sums_of(parts, high, keep, full)
+            for t in range(BLOCK // 128):
+                at = slice(c0 + t * 128, c0 + (t + 1) * 128)
+                stat_snd[it, 0:1, at] = high[t]
+                for j in range(len(sums) // len(high)):
+                    stat_snd[it, j + 1 : j + 2, at] = sums[j * len(high) + t]
         copies = [
             send(stat_snd.at[it], stat_rcv.at[it * (n_ref - 1) + k - 1], r_dev[k])
             for k in range(1, n_ref)
         ]
         for copy in copies:
             copy.wait_recv()
-        blocks = [stat_snd[it]] + [
-            stat_rcv[it * (n_ref - 1) + k - 1] for k in range(1, n_ref)
-        ]
+        blocks = [stat_snd[it]]
+        for k in range(1, n_ref):
+            theirs = stat_rcv[it * (n_ref - 1) + k - 1]
+            if paired:
+                theirs = jnp.concatenate([theirs[:, mine:], theirs[:, :mine]], axis=1)
+            blocks.append(theirs)
         high = functools.reduce(jnp.maximum, [blk[0:1] for blk in blocks])
-        scales = [jnp.exp(blk[0:1] - high) for blk in blocks]
+        scales = [jnp.exp2(blk[0:1] - high) for blk in blocks]
         sums = [
             functools.reduce(jnp.add, [blk[j : j + 1] * sc for blk, sc in zip(blocks, scales)])
             for j in ((1, 2, 3) if full else (1,))
         ]
         return high, sums
 
-    for it in range(ITERS):
-        high, (total, along, weight) = statistics(it, True)
-        vecs[0:1, :] = (along / total + prior_weight * prior_ref[...]) / (
-            weight / total + prior_weight
-        )
-    high, (total,) = statistics(ITERS, False)
-    vecs[1:2, :] = high
-    vecs[2:3, :] = vecs[0:1, :] / total
-    contrast_ref[...] = vecs[0:1, :]
-
-    def weigh(b, carry):
-        part = pl.ds(pl.multiple_of(b * LANES, LANES), LANES)
-        _, s = scored(part)
-        w[:, part] = (jnp.exp(s - vecs[1:2, part]) * vecs[2:3, part]).astype(BF16)
-        return carry
-
-    lax.fori_loop(0, n // LANES, weigh, 0)
+    def weigh(c0, width_):
+        slope, bend = coefficients(c0, width_)
+        tiles = range(width_ // 128)
+        top = [spread8(vecs[1:2, c0 + t * 128 : c0 + (t + 1) * 128]) for t in tiles]
+        gain = [spread8(vecs[2:3, c0 + t * 128 : c0 + (t + 1) * 128]) for t in tiles]
+
+        def body(r, carry):
+            rows_ = pl.ds(r, ROWS)
+            nrm = fold(norms[rows_, :])
+            for t in tiles:
+                at = slice(c0 + t * 128, c0 + (t + 1) * 128)
+                sc = slope[t][None] * fold(cross[rows_, at]) - bend[t][None] * nrm
+                e = jnp.exp2(sc - top[t][None]) * gain[t][None]
+                w[rows_, at] = e.reshape(ROWS, 128).astype(BF16)
+            return carry
+
+        over_rows(rows, body, 0)
+
+    if paired:
+        pcross, pnorms, given, taken = split
+        given[...] = jnp.zeros_like(given)
+
+
+        def score_slot(b):
+            im_copies[b].wait()
+            part = slice(b * LANES, (b + 1) * LANES)
+            cross[:, part] = lax.dot_general(
+                refs[...], im[part, :], nt, preferred_element_type=F32
+            )
+
+        handed = []
+        for b in range(mine // LANES, n // LANES):
+            score_slot(b)
+            if not handed:
+                pl.semaphore_wait(barrier, len(peers))
+                handed.append(send(norms, pnorms, r_dev[1]))
+            at = pl.ds((b - mine // LANES) * LANES, LANES)
+            handed.append(send(cross.at[:, pl.ds(b * LANES, LANES)], pcross.at[:, at], r_dev[1]))
+        for b in range(mine // LANES):
+            score_slot(b)
+        for copy in handed:
+            copy.wait_recv()
+        parts = [(cross, norms, 0), (pcross, pnorms, 0)]
+        tiles = mine // 128
+        for it in range(ITERS + 1):
+            high = scores(parts, 0, mine, keep)
+            sums = sums_of(parts, high, keep, it < ITERS)
+            for t in range(tiles):
+                at = slice(t * 128, (t + 1) * 128)
+                total = sums[t]
+                if it < ITERS:
+                    along, weight = sums[tiles + t], sums[2 * tiles + t]
+                    vecs[0:1, at] = (along / total + prior_weight * vecs[3:4, at]) / (
+                        weight / total + prior_weight
+                    )
+                else:
+                    a = vecs[0:1, at]
+                    vecs[1:2, at] = high[t]
+                    vecs[2:3, at] = a / total
+                    given[0:1, at] = a
+                    given[1:2, at] = high[t]
+                    given[2:3, at] = a / total
+        swap = send(given, taken, r_dev[1])
+        weigh(0, mine)
+        swap.wait_recv()
+        vecs[0:3, mine:n] = taken[0:3, :]
+        for k in range(n_ref):
+            contrast_ref[:, lanes_of(k)] = vecs[0:1, k * mine : (k + 1) * mine]
+        weigh(mine, mine)
+        for copy in handed:
+            copy.wait_send()
+            sent.remove(copy)
+    else:
+        for copy in im_copies:
+            copy.wait()
+        score_block(refs, 0, rows, None)
+        pl.semaphore_wait(barrier, len(peers))
+        for it in range(ITERS):
+            high, (total, along, weight) = statistics(it, True)
+            vecs[0:1, :] = (along / total + prior_weight * vecs[3:4, :]) / (
+                weight / total + prior_weight
+            )
+        high, (total,) = statistics(ITERS, False)
+        vecs[1:2, :] = high
+        vecs[2:3, :] = vecs[0:1, :] / total
+        contrast_ref[...] = vecs[0:1, :]
+        for c0 in range(0, n, BLOCK):
+            weigh(c0, BLOCK)
 
     def weighted(r0s, c0, store):
         def body(b, carry):
@@ -349,7 +498,12 @@
     score_block(gath, 0, 2 * qr, width ** (-0.5))
 
     high, (total,) = statistics(ITERS + 1, False)
-    loglik_ref[...] = high + jnp.log(total) - math.log(rows * n_ref)
+    loglik = high * math.log(2.0) + jnp.log(total) - math.log(rows * n_ref)
+    if paired:
+        for k in range(n_ref):
+            loglik_ref[:, lanes_of(k)] = loglik[:, k * mine : (k + 1) * mine]
+    else:
+        loglik_ref[...] = loglik
     for copy in outs:
         copy.wait()
     for copy in sent:
@@ -362,9 +516,18 @@
     rb = rows // (4 * nz)
     qr, half = nz * rb, width // 2
     steps = ITERS + 2
-    copies = steps * (n_ref - 1) + 6 * nz + 2 * (nz - 1) + (nz - 1) + 6 * nz
+    paired = n_ref == 2 and n % (2 * LANES) == 0
+    copies = 8 + steps * (n_ref - 1) + 6 * nz + 2 * (nz - 1) + (nz - 1) + 6 * nz
     peers = max(n_ref - 1, 1)
     flops = 6 * n * width * rows
+    split = []
+    if paired:
+        split = [
+            pltpu.VMEM((rows, n // 2), F32),
+            pltpu.VMEM((rows, 128), F32),
+            pltpu.VMEM((8, n // 2), F32),
+            pltpu.VMEM((8, n // 2), F32),
+        ]
     new_references, contrast, loglik = pl.pallas_call(
         functools.partial(kernel, nz, n_ref),
         out_shape=(
@@ -385,7 +548,7 @@
         scratch_shapes=[
             pltpu.VMEM((n, width), BF16),
             pltpu.VMEM((rows, width), BF16),
-            pltpu.VMEM((rows, LANES), F32),
+            pltpu.VMEM((rows, 128), F32),
             pltpu.VMEM((rows, n), F32),
             pltpu.VMEM((rows, n), BF16),
             pltpu.VMEM((4, qr, half), BF16),
@@ -399,6 +562,8 @@
             pltpu.VMEM((steps, 4, n), F32),
             pltpu.VMEM((steps * peers, 4, n), F32),
             pltpu.VMEM((8, n), F32),
+            pltpu.VMEM(((2 if paired else 1) * rows, BLOCK), F32),
+            *split,
             pltpu.SemaphoreType.DMA((n // LANES,)),
             pltpu.SemaphoreType.DMA((4 * nz,)),
             pltpu.SemaphoreType.DMA((4 * nz,)),

time: 75.7 us -> 76.3 us (level)
  no operation moved by 1% of the time
where the time goes in v1:
time: 76.3 us; the launch traced here: 76.1 us
  Pallas kernels  72.9 us (96%)
  local copies, waits for them, and re-layouts  2.51 us (3%)
    pallas_call x1, Pallas kernels, per_device(): pl.pallas_call(functools.partial(kernel, nz, n_ref), out_shape=(pltpu.VME...  72.9 us
    unnamed x3, local copies, waits for them, and re-layouts  2.51 us

profile of v1, /device:TPU:0, one launch (start us, length us, event | category | flops | bytes accessed | tf_op | source)
XLA Modules:
  0.0 76.1 jit_solution(12966231042914875859)
XLA Ops:
  0.6 72.9 %shard_map.58 = (bf16[512,2048]{1,0:T(8,128)(2,1)S(1)}, f32[1,1024]{1,0:T(1,128)S(1)}, f32[1,1024]{1,0:T(1,128)S(1)}) custom-call(bf16[1024,2048]{1,0:T(8,128)(2,1)} %im_hbm.1, bf16[512,2048]{1,0:T(8,128)(2,1)} %ref_hbm.1, f32[1,1024]{1,0:T(1,128)} %bitcast.5), custom_call_target="tpu_custom_call" | custom-call | flops 6442450944 | bytes 4194304 | tf_op jit(solution)/shard_map/pallas_call | solution.py:531
  73.6 1.3 %copy.9 = bf16[512,2048]{1,0:T(8,128)(2,1)} copy(bf16[512,2048]{1,0:T(8,128)(2,1)S(1)} %get-tuple-element.9) | data formatting | bytes 4194304
  74.9 0.6 copy.10
  75.5 0.6 copy.11

commit v2 on v0

--- a/solution.py
+++ b/solution.py
@@ -16,15 +16,20 @@
 
 MESH = pl.DeviceIdType.MESH
 LANES = 256
+BLOCK = 512
+TILES = BLOCK // 128
+ROWS = 64
+LOG2E = math.log2(math.e)
 QUADS = ((1, 0), (1, 1), (0, 1), (0, 0))
 F32 = jnp.float32
 BF16 = jnp.bfloat16
 
 
 def kernel(
-    nz, n_ref, im_hbm, ref_hbm, prior_ref, newref_hbm, contrast_ref, loglik_ref,
+    nz, n_ref, im_hbm, ref_hbm, prior_hbm, newref_hbm, contrast_ref, loglik_ref,
     im, refs, norms, cross, w, snd1, rcv1, acc, snd2, rcv2, snd3, rcv3, gath,
-    stat_snd, stat_rcv, vecs, im_sem, ref_sem, out_sem, ssem, rsem,
+    stat_snd, stat_rcv, vecs, keep, prior_sem,
+    stat_ssem, stat_rsem, im_sem, ref_sem, out_sem, ssem, rsem,
 ):
     n, width = im.shape
     rows = refs.shape[0]
@@ -60,6 +65,11 @@
     y_dev = {"img": chip(0, 1, 0)}
     z_dev = [{"img": chip(0, 0, k)} for k in range(nz)]
     r_dev = [{"ref": lax.rem(rme + k, n_ref)} for k in range(n_ref)]
+
+    barrier = pltpu.get_barrier_semaphore()
+    peers = r_dev[1:] + [x_dev, y_dev] + [z_dev[k] for k in range(1, nz) if k & (k - 1) == 0]
+    for dev in peers:
+        pl.semaphore_signal(barrier, inc=1, device_id=dev, device_id_type=MESH)
 
     ref_copies = []
     for q, (dx, dy) in enumerate(QUADS):
@@ -77,19 +87,15 @@
         copy = pltpu.make_async_copy(im_hbm.at[part], im.at[part], im_sem.at[b])
         copy.start()
         im_copies.append(copy)
-
-    barrier = pltpu.get_barrier_semaphore()
-    peers = [x_dev, y_dev] + [z_dev[k] for k in range(1, nz) if k & (k - 1) == 0] + r_dev[1:]
-    for dev in peers:
-        pl.semaphore_signal(barrier, inc=1, device_id=dev, device_id_type=MESH)
+    prior_copy = pltpu.make_async_copy(prior_hbm, vecs.at[3:4, :], prior_sem)
+    prior_copy.start()
 
     stat_snd[...] = jnp.zeros_like(stat_snd)
-    vecs[0:1, :] = prior_ref[...]
 
     def square_sums(source, r0, count, scale):
         block = source[r0 : r0 + count, :].astype(F32)
         total = jnp.sum(block * block, axis=1, keepdims=True) * scale
-        norms[r0 : r0 + count, :] = jnp.broadcast_to(total, (count, LANES))
+        norms[r0 : r0 + count, :] = jnp.broadcast_to(total, (count, 128))
 
     for s, copy in enumerate(ref_copies):
         copy.wait()
@@ -97,8 +103,6 @@
 
     nt = (((1,), (1,)), ((), ()))
     nn = (((1,), (0,)), ((), ()))
-    for copy in im_copies:
-        copy.wait()
 
     def score_block(source, r0, count, scale):
         def body(b, carry):
@@ -111,62 +115,162 @@
 
         lax.fori_loop(0, n // LANES, body, 0)
 
-    score_block(refs, 0, rows, None)
-    pl.semaphore_wait(barrier, len(peers))
-
-    def scored(part):
-        a = vecs[0:1, part]
-        c = cross[:, part]
-        return c, (sharpness * a) * c - ((0.5 * sharpness) * (a * a)) * norms[...]
-
-    def statistics(it, full):
-        def body(b, carry):
-            part = pl.ds(pl.multiple_of(b * LANES, LANES), LANES)
-            c, s = scored(part)
-            top = jnp.max(s, axis=0, keepdims=True)
-            e = jnp.exp(s - top)
-            stat_snd[it, 0:1, part] = top
-            stat_snd[it, 1:2, part] = jnp.sum(e, axis=0, keepdims=True)
-            if full:
-                stat_snd[it, 2:3, part] = jnp.sum(e * c, axis=0, keepdims=True)
-                stat_snd[it, 3:4, part] = jnp.sum(e * norms[...], axis=0, keepdims=True)
+    def fold(x):
+        return x.reshape(x.shape[0] // 8, 8, 128)
+
+    def spread8(x):
+        return jnp.broadcast_to(x, (8, 128))
+
+    def lanes(c0, width_=128):
+        return pl.ds(pl.multiple_of(c0, 128), width_)
+
+    def coefficients(c0, width_):
+        a = vecs[0:1, lanes(c0, width_)]
+        slope = (sharpness * LOG2E) * a
+        bend = (0.5 * sharpness * LOG2E) * (a * a)
+        tiles = range(0, width_, 128)
+        return (
+            [spread8(slope[:, t : t + 128]) for t in tiles],
+            [spread8(bend[:, t : t + 128]) for t in tiles],
+        )
+
+    def over_rows(count, body, init):
+        return lax.fori_loop(
+            0, count // ROWS, lambda i, c: body(pl.multiple_of(i * ROWS, ROWS), c), init
+        )
+
+    def scores(c0):
+        slope, bend = coefficients(c0, BLOCK)
+
+        def body(r, high):
+            part = pl.ds(r, ROWS)
+            nrm = fold(norms[part, :])
+            out = []
+            for t in range(TILES):
+                c = fold(cross[part, lanes(c0 + t * 128)])
+                sc = slope[t][None] * c - bend[t][None] * nrm
+                keep[part, t * 128 : (t + 1) * 128] = sc.reshape(ROWS, 128)
+                out.append(jnp.maximum(high[t], jnp.max(sc, axis=0)))
+            return tuple(out)
+
+        high = over_rows(rows, body, (jnp.full((8, 128), -jnp.inf, F32),) * TILES)
+        return [jnp.max(x, axis=0, keepdims=True) for x in high]
+
+    def sums_of(c0, high, full):
+        top = [spread8(x) for x in high]
+
+        def body(r, carry):
+            part = pl.ds(r, ROWS)
+            nrm = fold(norms[part, :]) if full else None
+            out = list(carry)
+            for t in range(TILES):
+                sc = fold(keep[part, t * 128 : (t + 1) * 128])
+                e = jnp.exp2(sc - top[t][None])
+                out[t] = out[t] + jnp.sum(e, axis=0)
+                if full:
+                    c = fold(cross[part, lanes(c0 + t * 128)])
+                    out[TILES + t] = out[TILES + t] + jnp.sum(e * c, axis=0)
+                    out[2 * TILES + t] = out[2 * TILES + t] + jnp.sum(e * nrm, axis=0)
+            return tuple(out)
+
+        zero = jnp.zeros((8, 128), F32)
+        carry = over_rows(rows, body, (zero,) * (TILES * (3 if full else 1)))
+        return [jnp.sum(x, axis=0, keepdims=True) for x in carry]
+
+    def weigh(c0):
+        slope, bend = coefficients(c0, BLOCK)
+        top = [spread8(vecs[1:2, lanes(c0 + t * 128)]) for t in range(TILES)]
+        gain = [spread8(vecs[2:3, lanes(c0 + t * 128)]) for t in range(TILES)]
+
+        def body(r, carry):
+            part = pl.ds(r, ROWS)
+            nrm = fold(norms[part, :])
+            for t in range(TILES):
+                at = lanes(c0 + t * 128)
+                sc = slope[t][None] * fold(cross[part, at]) - bend[t][None] * nrm
+                e = jnp.exp2(sc - top[t][None]) * gain[t][None]
+                w[part, at] = e.reshape(ROWS, 128).astype(BF16)
             return carry
 
-        lax.fori_loop(0, n // LANES, body, 0)
-        copies = [
-            send(stat_snd.at[it], stat_rcv.at[it * (n_ref - 1) + k - 1], r_dev[k])
-            for k in range(1, n_ref)
-        ]
-        for copy in copies:
-            copy.wait_recv()
-        blocks = [stat_snd[it]] + [
-            stat_rcv[it * (n_ref - 1) + k - 1] for k in range(1, n_ref)
-        ]
-        high = functools.reduce(jnp.maximum, [blk[0:1] for blk in blocks])
-        scales = [jnp.exp(blk[0:1] - high) for blk in blocks]
+        over_rows(rows, body, 0)
+
+    blocks = n // BLOCK
+
+    def stat_copy(it, h, k):
+        slot = (it * blocks + h) * (n_ref - 1) + k - 1
+        return pltpu.make_async_remote_copy(
+            src_ref=stat_snd.at[it, h], dst_ref=stat_rcv.at[slot],
+            send_sem=stat_ssem.at[slot], recv_sem=stat_rsem.at[slot],
+            device_id=r_dev[k], device_id_type=MESH,
+        )
+
+    def local_stats(it, h, full):
+        c0 = h * BLOCK
+        high = scores(c0)
+        sums = sums_of(c0, high, full)
+        for t in range(TILES):
+            at = slice(t * 128, (t + 1) * 128)
+            stat_snd[it, h, 0:1, at] = high[t]
+            for j in range(len(sums) // TILES):
+                stat_snd[it, h, j + 1 : j + 2, at] = sums[j * TILES + t]
+        for k in range(1, n_ref):
+            stat_copy(it, h, k).start()
+
+    def joint_stats(it, h, full):
+        shares = [stat_snd[it, h]]
+        for k in range(1, n_ref):
+            stat_copy(it, h, k).wait_recv()
+            shares.append(stat_rcv[(it * blocks + h) * (n_ref - 1) + k - 1])
+        high = functools.reduce(jnp.maximum, [share[0:1] for share in shares])
+        scales = [jnp.exp2(share[0:1] - high) for share in shares]
         sums = [
-            functools.reduce(jnp.add, [blk[j : j + 1] * sc for blk, sc in zip(blocks, scales)])
+            functools.reduce(
+                jnp.add, [share[j : j + 1] * sc for share, sc in zip(shares, scales)]
+            )
             for j in ((1, 2, 3) if full else (1,))
         ]
         return high, sums
 
-    for it in range(ITERS):
-        high, (total, along, weight) = statistics(it, True)
-        vecs[0:1, :] = (along / total + prior_weight * prior_ref[...]) / (
+    def each(count, body):
+        def step(i, carry):
+            body(i)
+            return carry
+
+        lax.fori_loop(0, count, step, 0)
+
+
+    prior_copy.wait()
+    vecs[0:1, :] = vecs[3:4, :]
+
+    def first_cross(b):
+        part = pl.ds(pl.multiple_of(b * LANES, LANES), LANES)
+        pltpu.make_async_copy(im_hbm.at[part], im.at[part], im_sem.at[b]).wait()
+        cross[:, part] = lax.dot_general(
+            refs[...], im[part, :], nt, preferred_element_type=F32
+        )
+
+    def refit(i):
+        it, h = i // blocks, lax.rem(i, blocks)
+        at = lanes(h * BLOCK, BLOCK)
+        _, (total, along, weight) = joint_stats(it, h, True)
+        vecs[0:1, at] = (along / total + prior_weight * vecs[3:4, at]) / (
             weight / total + prior_weight
         )
-    high, (total,) = statistics(ITERS, False)
-    vecs[1:2, :] = high
-    vecs[2:3, :] = vecs[0:1, :] / total
+        local_stats(it + 1, h, True)
+
+    def settle(h):
+        at = lanes(h * BLOCK, BLOCK)
+        high, (total,) = joint_stats(ITERS, h, False)
+        vecs[1:2, at] = high
+        vecs[2:3, at] = vecs[0:1, at] / total
+        weigh(h * BLOCK)
+
+    each(n // LANES, first_cross)
+    pl.semaphore_wait(barrier, len(peers))
+    each(blocks, lambda h: local_stats(0, h, True))
+    each(ITERS * blocks, refit)
+    each(blocks, settle)
     contrast_ref[...] = vecs[0:1, :]
-
-    def weigh(b, carry):
-        part = pl.ds(pl.multiple_of(b * LANES, LANES), LANES)
-        _, s = scored(part)
-        w[:, part] = (jnp.exp(s - vecs[1:2, part]) * vecs[2:3, part]).astype(BF16)
-        return carry
-
-    lax.fori_loop(0, n // LANES, weigh, 0)
 
     def weighted(r0s, c0, store):
         def body(b, carry):
@@ -348,8 +452,19 @@
     finish(1)
     score_block(gath, 0, 2 * qr, width ** (-0.5))
 
-    high, (total,) = statistics(ITERS + 1, False)
-    loglik_ref[...] = high + jnp.log(total) - math.log(rows * n_ref)
+    def final_likelihood(h):
+        high, (total,) = joint_stats(ITERS + 1, h, False)
+        loglik_ref[:, lanes(h * BLOCK, BLOCK)] = (
+            high * math.log(2.0) + jnp.log(total) - math.log(rows * n_ref)
+        )
+
+    each(blocks, lambda h: local_stats(ITERS + 1, h, False))
+    each(blocks, final_likelihood)
+    for k in range(1, n_ref):
+        each(
+            (ITERS + 2) * blocks,
+            lambda i: stat_copy(i // blocks, lax.rem(i, blocks), k).wait_send(),
+        )
     for copy in outs:
         copy.wait()
     for copy in sent:
@@ -362,8 +477,9 @@
     rb = rows // (4 * nz)
     qr, half = nz * rb, width // 2
     steps = ITERS + 2
-    copies = steps * (n_ref - 1) + 6 * nz + 2 * (nz - 1) + (nz - 1) + 6 * nz
     peers = max(n_ref - 1, 1)
+    stat_copies = steps * (n // BLOCK) * peers
+    copies = 6 * nz + 2 * (nz - 1) + (nz - 1) + 6 * nz
     flops = 6 * n * width * rows
     new_references, contrast, loglik = pl.pallas_call(
         functools.partial(kernel, nz, n_ref),
@@ -375,7 +491,7 @@
         in_specs=[
             pl.BlockSpec(memory_space=pl.ANY),
             pl.BlockSpec(memory_space=pl.ANY),
-            pl.BlockSpec(memory_space=pltpu.VMEM),
+            pl.BlockSpec(memory_space=pl.ANY),
         ],
         out_specs=(
             pl.BlockSpec(memory_space=pltpu.VMEM),
@@ -385,7 +501,7 @@
         scratch_shapes=[
             pltpu.VMEM((n, width), BF16),
             pltpu.VMEM((rows, width), BF16),
-            pltpu.VMEM((rows, LANES), F32),
+            pltpu.VMEM((rows, 128), F32),
             pltpu.VMEM((rows, n), F32),
             pltpu.VMEM((rows, n), BF16),
             pltpu.VMEM((4, qr, half), BF16),
@@ -396,9 +512,13 @@
             pltpu.VMEM((2, max(nz - 1, 1), rb, half), BF16),
             pltpu.VMEM((2, max(nz - 1, 1), rb, half), BF16),
             pltpu.VMEM((rows, width), BF16),
-            pltpu.VMEM((steps, 4, n), F32),
-            pltpu.VMEM((steps * peers, 4, n), F32),
+            pltpu.VMEM((steps, n // BLOCK, 4, BLOCK), F32),
+            pltpu.VMEM((stat_copies, 4, BLOCK), F32),
             pltpu.VMEM((8, n), F32),
+            pltpu.VMEM((rows, BLOCK), F32),
+            pltpu.SemaphoreType.DMA(()),
+            pltpu.SemaphoreType.DMA((stat_copies,)),
+            pltpu.SemaphoreType.DMA((stat_copies,)),
             pltpu.SemaphoreType.DMA((n // LANES,)),
             pltpu.SemaphoreType.DMA((4 * nz,)),
             pltpu.SemaphoreType.DMA((4 * nz,)),

time: 75.7 us -> 73.4 us (0.970)
  Pallas kernels: 72.4 us -> 70.1 us
    pallas_call x1, Pallas kernels: 72.4 us -> 70.1 us  [per_device(): pl.pallas_call(functools.partial(kernel, nz, n_ref), out_shape=(pltpu.VME...]
where the time goes in v2:
time: 73.4 us; the launch traced here: 73.3 us
  Pallas kernels  70.1 us (96%)
  local copies, waits for them, and re-layouts  2.51 us (3%)
    pallas_call x1, Pallas kernels, per_device(): pl.pallas_call(functools.partial(kernel, nz, n_ref), out_shape=(pltpu.VME...  70.1 us
    unnamed x3, local copies, waits for them, and re-layouts  2.51 us

profile of v2, /device:TPU:0, one launch (start us, length us, event | category | flops | bytes accessed | tf_op | source)
XLA Modules:
  0.0 73.3 jit_solution(17020570447277152069)
XLA Ops:
  0.6 70.1 %shard_map.58 = (bf16[512,2048]{1,0:T(8,128)(2,1)S(1)}, f32[1,1024]{1,0:T(1,128)S(1)}, f32[1,1024]{1,0:T(1,128)S(1)}) custom-call(bf16[1024,2048]{1,0:T(8,128)(2,1)} %im_hbm.1, bf16[512,2048]{1,0:T(8,128)(2,1)} %ref_hbm.1, f32[1,1024]{1,0:T(1,128)} %bitcast.5), custom_call_target="tpu_custom_call" | custom-call | flops 6442450944 | bytes 4194304 | tf_op jit(solution)/shard_map/pallas_call | solution.py:484
  70.8 1.3 %copy.9 = bf16[512,2048]{1,0:T(8,128)(2,1)} copy(bf16[512,2048]{1,0:T(8,128)(2,1)S(1)} %get-tuple-element.9) | data formatting | bytes 4194304
  72.1 0.6 copy.10
  72.7 0.6 copy.11

commit v3 on v2

v3 whole, which is shorter than its diff:
```python
import functools
import math

import jax
import jax.numpy as jnp
from jax import lax
from jax.experimental import pallas as pl
from jax.experimental.pallas import tpu as pltpu
from jax.sharding import PartitionSpec as P

ITERS = 3

sharpness = 2.0
prior_weight = 1.0
epsilon = 1e-06

MESH = pl.DeviceIdType.MESH
LANES = 256
BLOCK = 512
TILES = BLOCK // 128
ROWS = 64
LOG2E = math.log2(math.e)
QUADS = ((1, 0), (1, 1), (0, 1), (0, 0))
F32 = jnp.float32
BF16 = jnp.bfloat16

RATE = 46.5e3
HOP = 2.1
FAR = 0.6
BACKLOG = 0.5
STEP = 0.12
SCORE = 0.5
PIECES = 2


def plan(groups, nz, block, pieces):
    unit = block / RATE
    zs = range(1, nz)
    todo = {}
    for g in range(groups):
        for s in (0, 1):
            for j in (0, 1):
                todo["S1", g, s, j] = (2, g, 0), (), [(("s1", g, s, j), "xy"[s], unit * nz)]
            todo["S2", g, s] = (
                (1, g, 0), [("s1", g, s, 0)], [(("s2", g, s), "yx"[s], unit * nz)]
            )
        met = [("s1", g, s, 1) for s in (0, 1)] + [("s2", g, s) for s in (0, 1)]
        met_z = [("z", g, k) for k in zs]
        weight = {k: 2 * unit * (1.0 if k == 1 else 1.5) for k in zs}
        todo["Z", g] = (0, g, 0), met, [(("z", g, k), "z", weight[k]) for k in zs]
        todo["A", g] = (0, g, 0), met + met_z, [(("az", g, k), "z", weight[k]) for k in zs]
        every = []
        for k in range(nz):
            base = [("az", g, k)] if k else [("A", g)]
            outs = [[(("y", g, k, 0), "y", unit), (("x", g, k, 1), "x", unit)]]
            outs.append([(("y", g, k, 1), "y", unit), (("x", g, k, 0), "x", unit)])
            outs.append([(("fx", g, k), "x", unit), (("fy", g, k), "y", unit)])
            todo["P", g, k] = (4, g, 0), base, outs[0]
            todo["F", g, k] = (4, g, 1), [("y", g, k, 0), ("x", g, k, 1)], outs[1 + 1]
            todo["Q", g, k] = (4, g, 2), base, outs[1]
            every += [name for out in outs for name, _, _ in out]
        for p in range(pieces):
            todo["G", g, p] = (5, g, p), every, []
    clock, order, arrived = 0.0, [], {}
    free = dict.fromkeys("xyz", 0.0)
    while todo:
        best = None
        for name, (rank, waits, out) in todo.items():
            if all(wait in arrived for wait in waits):
                start = max([arrived[wait] for wait in waits], default=0.0)
                start = max([start, clock] + [free[link] - BACKLOG for _, link, _ in out])
                if best is None or (start, rank, name) < best:
                    best = (start, rank, name)
        start, _, name = best
        out = todo.pop(name)[2]
        clock = start + (SCORE if name[0] == "G" else STEP)
        arrived[name] = clock
        for message, link, length in out:
            free[link] = max(free[link], clock) + length
            arrived[message] = free[link] + HOP
            if link == "z" and message[2] > 1:
                arrived[message] += FAR
        order.append(name)
    return order


def kernel(
    nz, n_ref, im_hbm, ref_hbm, prior_hbm, newref, contrast_ref, loglik_ref,
    im, refs, norms, cross, w, snd1, rcv1, acc, snd2, rcv2, snd3, rcv3, own,
    stat_snd, stat_rcv, vecs, keep, prior_sem,
    stat_ssem, stat_rsem, im_sem, ref_sem, ssem, rsem,
):
    n, width = im.shape
    rows = refs.shape[0]
    groups = own.shape[0]
    rg = own.shape[1]
    gr = nz * rg
    qr = groups * gr
    half = width // 2
    me = lax.axis_index("img")
    rme = lax.axis_index("ref")
    x, y, z = lax.rem(me, 2), lax.rem(me // 2, 2), me // 4
    def chip(dx, dy, dz):
        zz, bit = z, 1
        while bit < nz:
            if dz & bit:
                zz = zz + bit - 2 * bit * lax.rem(z // bit, 2)
            bit *= 2
        return zz * 4 + lax.rem(y + dy, 2) * 2 + lax.rem(x + dx, 2)

    def send(src, dst, dev, kind, slot):
        pltpu.make_async_remote_copy(
            src_ref=src, dst_ref=dst, send_sem=ssem.at[kind], recv_sem=rsem.at[slot],
            device_id=dev, device_id_type=MESH,
        ).start()

    x_dev = {"img": chip(1, 0, 0)}
    y_dev = {"img": chip(0, 1, 0)}
    z_dev = [{"img": chip(0, 0, k)} for k in range(nz)]
    r_dev = [{"ref": lax.rem(rme + k, n_ref)} for k in range(n_ref)]

    barrier = pltpu.get_barrier_semaphore()
    peers = r_dev[1:] + [x_dev, y_dev] + z_dev[1:]
    for dev in peers:
        pl.semaphore_signal(barrier, inc=1, device_id=dev, device_id_type=MESH)

    ref_copies = []
    per_ref = rows // ref_sem.shape[0]
    for s in range(ref_sem.shape[0]):
        part = pl.ds(s * per_ref, per_ref)
        copy = pltpu.make_async_copy(ref_hbm.at[part], refs.at[part], ref_sem.at[s])
        copy.start()
        ref_copies.append(copy)
    for b in range(n // LANES):
        part = pl.ds(b * LANES, LANES)
        pltpu.make_async_copy(im_hbm.at[part], im.at[part], im_sem.at[b]).start()
    prior_copy = pltpu.make_async_copy(prior_hbm, vecs.at[3:4, :], prior_sem)
    prior_copy.start()

    stat_snd[...] = jnp.zeros_like(stat_snd)

    def square_sums(source, r0, count, scale):
        block = source[pl.ds(r0, count), :].astype(F32)
        total = jnp.sum(block * block, axis=1, keepdims=True) * scale
        norms[pl.ds(r0, count), :] = jnp.broadcast_to(total, (count, 128))

    for s, copy in enumerate(ref_copies):
        copy.wait()
        for r0 in range(s * per_ref, (s + 1) * per_ref, 32):
            square_sums(refs, r0, 32, 1.0)

    nt = (((1,), (1,)), ((), ()))
    nn = (((1,), (0,)), ((), ()))

    def fold(x):
        return x.reshape(x.shape[0] // 8, 8, 128)

    def spread8(x):
        return jnp.broadcast_to(x, (8, 128))

    at_chip = {
        (dx, dy, dz): chip(dx, dy, dz) * rg for dx, dy in QUADS for dz in range(nz)
    }

    def row0(g, where):
        return pl.multiple_of(g * (4 * gr) + at_chip[where], 8)

    def lanes(c0, width_=128):
        return pl.ds(pl.multiple_of(c0, 128), width_)

    def coefficients(c0, width_):
        a = vecs[0:1, lanes(c0, width_)]
        slope = (sharpness * LOG2E) * a
        bend = (0.5 * sharpness * LOG2E) * (a * a)
        tiles = range(0, width_, 128)
        return (
            [spread8(slope[:, t : t + 128]) for t in tiles],
            [spread8(bend[:, t : t + 128]) for t in tiles],
        )

    def over_rows(count, body, init):
        return lax.fori_loop(
            0, count // ROWS, lambda i, c: body(pl.multiple_of(i * ROWS, ROWS), c), init
        )

    def scores(c0):
        slope, bend = coefficients(c0, BLOCK)

        def body(r, high):
            part = pl.ds(r, ROWS)
            nrm = fold(norms[part, :])
            out = []
            for t in range(TILES):
                c = fold(cross[part, lanes(c0 + t * 128)])
                sc = slope[t][None] * c - bend[t][None] * nrm
                keep[part, t * 128 : (t + 1) * 128] = sc.reshape(ROWS, 128)
                out.append(jnp.maximum(high[t], jnp.max(sc, axis=0)))
            return tuple(out)

        high = over_rows(rows, body, (jnp.full((8, 128), -jnp.inf, F32),) * TILES)
        return [jnp.max(x, axis=0, keepdims=True) for x in high]

    def sums_of(c0, high, full):
        top = [spread8(x) for x in high]

        def body(r, carry):
            part = pl.ds(r, ROWS)
            nrm = fold(norms[part, :]) if full else None
            out = list(carry)
            for t in range(TILES):
                sc = fold(keep[part, t * 128 : (t + 1) * 128])
                e = jnp.exp2(sc - top[t][None])
                out[t] = out[t] + jnp.sum(e, axis=0)
                if full:
                    c = fold(cross[part, lanes(c0 + t * 128)])
                    out[TILES + t] = out[TILES + t] + jnp.sum(e * c, axis=0)
                    out[2 * TILES + t] = out[2 * TILES + t] + jnp.sum(e * nrm, axis=0)
            return tuple(out)

        zero = jnp.zeros((8, 128), F32)
        carry = over_rows(rows, body, (zero,) * (TILES * (3 if full else 1)))
        return [jnp.sum(x, axis=0, keepdims=True) for x in carry]

    def weigh(c0):
        slope, bend = coefficients(c0, BLOCK)
        top = [spread8(vecs[1:2, lanes(c0 + t * 128)]) for t in range(TILES)]
        gain = [spread8(vecs[2:3, lanes(c0 + t * 128)]) for t in range(TILES)]

        def body(g, carry):
            for q in range(4):
                parts = [pl.ds(row0(g, QUADS[q] + (dz,)), rg) for dz in range(nz)]
                nrm = [norms[part, :].reshape(rg // 8, 8, 128) for part in parts]
                to = pl.ds(pl.multiple_of(q * qr + g * gr, 8), gr)
                for t in range(TILES):
                    at = lanes(c0 + t * 128)
                    e = []
                    for part, norm in zip(parts, nrm):
                        c = cross[part, at].reshape(rg // 8, 8, 128)
                        sc = slope[t][None] * c - bend[t][None] * norm
                        e.append((jnp.exp2(sc - top[t][None]) * gain[t][None]).reshape(rg, 128))
                    w[to, at] = jnp.concatenate(e, axis=0).astype(BF16)
            return carry

        lax.fori_loop(0, groups, body, 0)

    blocks = n // BLOCK

    def stat_copy(it, h, k):
        slot = (it * blocks + h) * (n_ref - 1) + k - 1
        return pltpu.make_async_remote_copy(
            src_ref=stat_snd.at[it, h], dst_ref=stat_rcv.at[slot],
            send_sem=stat_ssem.at[k - 1],
            recv_sem=stat_rsem.at[(lax.rem(it, 2) * blocks + h) * (n_ref - 1) + k - 1],
            device_id=r_dev[k], device_id_type=MESH,
        )

    def local_stats(it, h, full):
        c0 = h * BLOCK
        high = scores(c0)
        sums = sums_of(c0, high, full)
        for t in range(TILES):
            at = slice(t * 128, (t + 1) * 128)
            stat_snd[it, h, 0:1, at] = high[t]
            for j in range(len(sums) // TILES):
                stat_snd[it, h, j + 1 : j + 2, at] = sums[j * TILES + t]
        for k in range(1, n_ref):
            stat_copy(it, h, k).start()

    def joint_stats(it, h, full):
        shares = [stat_snd[it, h]]
        for k in range(1, n_ref):
            stat_copy(it, h, k).wait_recv()
            shares.append(stat_rcv[(it * blocks + h) * (n_ref - 1) + k - 1])
        high = functools.reduce(jnp.maximum, [share[0:1] for share in shares])
        scales = [jnp.exp2(share[0:1] - high) for share in shares]
        sums = [
            functools.reduce(
                jnp.add, [share[j : j + 1] * sc for share, sc in zip(shares, scales)]
            )
            for j in ((1, 2, 3) if full else (1,))
        ]
        return high, sums

    def each(count, body):
        def step(i, carry):
            body(i)
            return carry

        lax.fori_loop(0, count, step, 0)


    prior_copy.wait()
    vecs[0:1, :] = vecs[3:4, :]

    def first_cross(b):
        part = pl.ds(pl.multiple_of(b * LANES, LANES), LANES)
        pltpu.make_async_copy(im_hbm.at[part], im.at[part], im_sem.at[b]).wait()
        cross[:, part] = lax.dot_general(
            refs[...], im[part, :], nt, preferred_element_type=F32
        )

    def refit(i):
        it, h = i // blocks, lax.rem(i, blocks)
        at = lanes(h * BLOCK, BLOCK)
        _, (total, along, weight) = joint_stats(it, h, True)
        vecs[0:1, at] = (along / total + prior_weight * vecs[3:4, at]) / (
            weight / total + prior_weight
        )
        local_stats(it + 1, h, True)

    def settle(h):
        at = lanes(h * BLOCK, BLOCK)
        high, (total,) = joint_stats(ITERS, h, False)
        vecs[1:2, at] = high
        vecs[2:3, at] = vecs[0:1, at] / total
        weigh(h * BLOCK)

    each(n // LANES, first_cross)
    pl.semaphore_wait(barrier, len(peers))
    each(blocks, lambda h: local_stats(0, h, True))
    each(ITERS * blocks, refit)
    each(blocks, settle)
    contrast_ref[...] = vecs[0:1, :]

    def weighted(r0s, c0, store):
        def body(b, carry):
            col = pl.multiple_of(b * LANES, LANES)
            lhs = [w[r0 : r0 + cnt, :] for r0, cnt in r0s]
            lhs = lhs[0] if len(lhs) == 1 else jnp.concatenate(lhs, axis=0)
            rhs = im[:, pl.ds(pl.multiple_of(c0 + col, LANES), LANES)]
            out = lax.dot_general(lhs, rhs, nn, preferred_element_type=F32)
            store(pl.ds(col, LANES), out[:qr], out[qr:])
            return carry

        lax.fori_loop(0, half // LANES, body, 0)

    def to_send(stream, first_is_far):
        def store(cols, lo, hi):
            far, near = (lo, hi) if first_is_far else (hi, lo)
            snd1[stream * 2, :, cols] = far.astype(BF16)
            snd1[stream * 2 + 1, :, cols] = near.astype(BF16)

        return store

    def to_keep(stream):
        def store(cols, lo, hi):
            acc[stream * 2, :, cols] = lo
            acc[stream * 2 + 1, :, cols] = hi

        return store

    hop_dev = (x_dev, y_dev)
    landed = set()
    kinds = {"s1": 0, "s2": 1, "z": 2, "az": 3, "y": 4, "x": 4, "fx": 5, "fy": 5}
    per_group = 2 + 1 + (nz - 1) + 2 * nz + 2

    def slot_of(name):
        kind, g = name[:2]
        if kind == "s1" and name[3] == 0:
            at = name[2]
        elif kind in ("s1", "s2"):
            at = 2
        elif kind == "z":
            at = 3
        elif kind == "az":
            at = 3 + name[2]
        elif kind in ("x", "y") and name[3] == (kind == "x"):
            at = 3 + nz + 2 * name[2] + (kind == "x")
        else:
            at = 3 + 3 * nz
        return g * per_group + at

    def put(name, src, dst, dev):
        send(src, dst, dev, kinds[name[0]], slot_of(name))

    def arrive(name, like):
        slot = slot_of(name)
        if slot not in landed:
            landed.add(slot)
            pltpu.make_async_copy(like, like, rsem.at[slot]).wait()

    def send1(g, s, j):
        part = pl.ds(g * gr, gr)
        put(("s1", g, s, j), snd1.at[s * 2 + j, part], rcv1.at[s * 2 + j, part], hop_dev[s])

    def send2(g, s):
        part = pl.ds(g * gr, gr)
        arrive(("s1", g, s, 0), rcv1.at[s * 2, part])
        snd2[s, part, :] = (acc[s * 2, part, :] + rcv1[s * 2, part, :].astype(F32)).astype(BF16)
        put(("s2", g, s), snd2.at[s, part], rcv2.at[s, part], hop_dev[1 - s])

    def send3(g):
        part = pl.ds(g * gr, gr)
        arrive(("s2", g, 0), rcv1.at[:, part])
        for s in (0, 1):
            total = (
                acc[s * 2 + 1, part, :]
                + rcv1[s * 2 + 1, part, :].astype(F32)
                + rcv2[s, part, :].astype(F32)
            )
            cols = slice(s * half, (s + 1) * half)
            own[g, :, cols] = total[0:rg]
            for k in range(1, nz):
                snd3[g, k - 1, :, cols] = total[k * rg : (k + 1) * rg].astype(BF16)
        for k in range(1, nz):
            put(("z", g, k), snd3.at[g, k - 1], rcv3.at[g, k - 1], z_dev[k])

    def finish(g):
        total = own[g]
        if nz > 1:
            arrive(("z", g, 1), rcv3.at[g])
        for k in range(1, nz):
            total = total + rcv3[g, k - 1].astype(F32)
        square = jnp.sum(total * total, axis=1, keepdims=True)
        mine = pl.ds(row0(g, (0, 0, 0)), rg)
        newref[mine, :] = (total * lax.rsqrt(square / width + epsilon)).astype(BF16)
        for k in range(1, nz):
            put(("az", g, k), newref.at[mine], newref.at[mine], z_dev[k])

    def piece(g, where, side):
        return newref.at[pl.ds(row0(g, where), rg), pl.ds(side * half, half)]

    def pass_on(name, g, where, side, dev):
        part = piece(g, where, side)
        put(name, part, part, dev)

    def spread_first(g, k):
        if k:
            arrive(("az", g, k), newref.at[pl.ds(row0(g, (0, 0, k)), rg)])
        pass_on(("y", g, k, 0), g, (0, 0, k), 0, y_dev)
        pass_on(("x", g, k, 1), g, (0, 0, k), 1, x_dev)

    def spread_second(g, k):
        if k:
            arrive(("az", g, k), newref.at[pl.ds(row0(g, (0, 0, k)), rg)])
        pass_on(("y", g, k, 1), g, (0, 0, k), 1, y_dev)
        pass_on(("x", g, k, 0), g, (0, 0, k), 0, x_dev)

    def forward(g, k):
        arrive(("y", g, k, 0), piece(g, (0, 1, k), 0))
        pass_on(("fx", g, k), g, (0, 1, k), 0, x_dev)
        arrive(("x", g, k, 1), piece(g, (1, 0, k), 1))
        pass_on(("fy", g, k), g, (1, 0, k), 1, y_dev)

    def score_group(g, p):
        r0, count = g * 4 * gr, 4 * gr
        if p == 0:
            arrive(("fx", g, 0), newref.at[pl.ds(r0, 2 * gr)])

            def squares(i):
                square_sums(newref, pl.multiple_of(r0 + i * 32, 32), 32, 1.0 / width)

            each(count // 32, squares)

        def body(i):
            part = pl.ds(pl.multiple_of((p * per_piece + i) * LANES, LANES), LANES)
            out = lax.dot_general(
                newref[r0 : r0 + count, :], im[part, :], nt, preferred_element_type=F32
            )
            cross[r0 : r0 + count, part] = out * width ** (-0.5)

        each(per_piece, body)

    per_piece = n // LANES // PIECES
    steps = {
        "S1": send1, "S2": send2, "Z": send3, "A": finish, "P": spread_first,
        "Q": spread_second, "F": forward, "G": score_group,
    }
    order = plan(groups, nz, rg * width, PIECES)
    first = [name for name in order if name[0] == "S1" and name[1] < 2]
    rest = [name for name in order if name not in first]

    weighted([(0, 2 * qr)], 0, to_send(0, False))
    for name in first:
        if name[2] == 0:
            send1(*name[1:])
    weighted([(qr, 2 * qr)], half, to_send(1, True))
    for name in first:
        if name[2] == 1:
            send1(*name[1:])
    weighted([(2 * qr, 2 * qr)], 0, to_keep(0))
    weighted([(0, qr), (3 * qr, qr)], half, to_keep(1))
    for name in rest:
        steps[name[0]](*name[1:])

    def final_likelihood(h):
        high, (total,) = joint_stats(ITERS + 1, h, False)
        loglik_ref[:, lanes(h * BLOCK, BLOCK)] = (
            high * math.log(2.0) + jnp.log(total) - math.log(rows * n_ref)
        )

    each(blocks, lambda h: local_stats(ITERS + 1, h, False))
    each(blocks, final_likelihood)
    def all_sent(like, sem):
        pltpu.make_async_copy(like, like, sem).wait()

    for k in range(1, n_ref):
        all_sent(stat_snd, stat_ssem.at[k - 1])
    for kind, like in enumerate((snd1, snd2, snd3, snd3)):
        all_sent(like, ssem.at[kind])
    all_sent(newref.at[pl.ds(0, 2 * qr)], ssem.at[4])
    all_sent(newref.at[pl.ds(0, qr)], ssem.at[5])


def per_device(nz, n_ref, images, references, initial_contrast):
    n, width = images.shape
    rows = references.shape[0]
    groups = max(1, min(4, rows // (32 * nz)))
    rg = rows // (4 * nz * groups)
    qr, half = nz * rg * groups, width // 2
    steps = ITERS + 2
    peers = max(n_ref - 1, 1)
    stat_copies = steps * (n // BLOCK) * peers
    arrivals = groups * (2 + 1 + (nz - 1) + 2 * nz + 2)
    flops = 6 * n * width * rows
    new_references, contrast, loglik = pl.pallas_call(
        functools.partial(kernel, nz, n_ref),
        out_shape=(
            pltpu.VMEM((rows, width), BF16),
            pltpu.VMEM((1, n), F32),
            pltpu.VMEM((1, n), F32),
        ),
        in_specs=[
            pl.BlockSpec(memory_space=pl.ANY),
            pl.BlockSpec(memory_space=pl.ANY),
            pl.BlockSpec(memory_space=pl.ANY),
        ],
        out_specs=(
            pl.BlockSpec(memory_space=pltpu.VMEM),
            pl.BlockSpec(memory_space=pltpu.VMEM),
            pl.BlockSpec(memory_space=pltpu.VMEM),
        ),
        scratch_shapes=[
            pltpu.VMEM((n, width), BF16),
            pltpu.VMEM((rows, width), BF16),
            pltpu.VMEM((rows, 128), F32),
            pltpu.VMEM((rows, n), F32),
            pltpu.VMEM((rows, n), BF16),
            pltpu.VMEM((4, qr, half), BF16),
            pltpu.VMEM((4, qr, half), BF16),
            pltpu.VMEM((4, qr, half), F32),
            pltpu.VMEM((2, qr, half), BF16),
            pltpu.VMEM((2, qr, half), BF16),
            pltpu.VMEM((groups, max(nz - 1, 1), rg, width), BF16),
            pltpu.VMEM((groups, max(nz - 1, 1), rg, width), BF16),
            pltpu.VMEM((groups, rg, width), F32),
            pltpu.VMEM((steps, n // BLOCK, 4, BLOCK), F32),
            pltpu.VMEM((stat_copies, 4, BLOCK), F32),
            pltpu.VMEM((8, n), F32),
            pltpu.VMEM((rows, BLOCK), F32),
            pltpu.SemaphoreType.DMA(()),
            pltpu.SemaphoreType.DMA((peers,)),
            pltpu.SemaphoreType.DMA((2 * (n // BLOCK) * peers,)),
            pltpu.SemaphoreType.DMA((n // LANES,)),
            pltpu.SemaphoreType.DMA((4,)),
            pltpu.SemaphoreType.DMA((6,)),
            pltpu.SemaphoreType.DMA((arrivals,)),
        ],
        compiler_params=pltpu.CompilerParams(
            collective_id=0, has_side_effects=True, vmem_limit_bytes=56 * 1024 * 1024
        ),
        cost_estimate=pl.CostEstimate(
            flops=flops, bytes_accessed=2 * n * width, transcendentals=0
        ),
    )(images, references, initial_contrast[None, :])
    return (new_references, contrast[0], loglik[0])


def solution(mesh):
    n_img, n_ref = mesh.shape["img"], mesh.shape["ref"]
    placed = (P("img", None), P("ref", None), P("img"))
    return jax.shard_map(
        functools.partial(per_device, n_img // 4, n_ref),
        mesh=mesh,
        in_specs=placed,
        out_specs=(P("ref", None), P("img"), P("img")),
        check_vma=False,
    )
```

time: 73.4 us -> 70.9 us (0.966)
  Pallas kernels: 70.1 us -> 67.6 us
    pallas_call x1, Pallas kernels: 70.1 us -> 67.6 us  [per_device(): pl.pallas_call(functools.partial(kernel, nz, n_ref), out_shape=(pltpu.VME...]
where the time goes in v3:
time: 70.9 us; the launch traced here: 70.8 us
  Pallas kernels  67.6 us (95%)
  local copies, waits for them, and re-layouts  2.51 us (4%)
    pallas_call x1, Pallas kernels, per_device(): pl.pallas_call(functools.partial(kernel, nz, n_ref), out_shape=(pltpu.VME...  67.6 us
    unnamed x3, local copies, waits for them, and re-layouts  2.51 us

profile of v3, /device:TPU:0, one launch (start us, length us, event | category | flops | bytes accessed | tf_op | source)
XLA Modules:
  0.0 70.8 jit_solution(13644814471731338027)
XLA Ops:
  0.6 67.6 %shard_map.58 = (bf16[512,2048]{1,0:T(8,128)(2,1)S(1)}, f32[1,1024]{1,0:T(1,128)S(1)}, f32[1,1024]{1,0:T(1,128)S(1)}) custom-call(bf16[1024,2048]{1,0:T(8,128)(2,1)} %im_hbm.1, bf16[512,2048]{1,0:T(8,128)(2,1)} %ref_hbm.1, f32[1,1024]{1,0:T(1,128)} %bitcast.5), custom_call_target="tpu_custom_call" | custom-call | flops 6442450944 | bytes 4194304 | tf_op jit(solution)/shard_map/pallas_call | solution.py:516
  68.3 1.3 %copy.9 = bf16[512,2048]{1,0:T(8,128)(2,1)} copy(bf16[512,2048]{1,0:T(8,128)(2,1)S(1)} %get-tuple-element.9) | data formatting | bytes 4194304
  69.6 0.6 copy.10
  70.2 0.6 copy.11

commit v4 on v3

--- a/solution.py
+++ b/solution.py
@@ -18,7 +18,7 @@
 LANES = 256
 BLOCK = 512
 TILES = BLOCK // 128
-ROWS = 64
+ROWS = 128
 LOG2E = math.log2(math.e)
 QUADS = ((1, 0), (1, 1), (0, 1), (0, 0))
 F32 = jnp.float32
@@ -29,11 +29,11 @@
 FAR = 0.6
 BACKLOG = 0.5
 STEP = 0.12
-SCORE = 0.5
-PIECES = 2
-
-
-def plan(groups, nz, block, pieces):
+SCORE = 0.6
+PAIR = 2
+
+
+def plan(groups, nz, block, pieces, pair):
     unit = block / RATE
     zs = range(1, nz)
     todo = {}
@@ -59,8 +59,10 @@
             todo["F", g, k] = (4, g, 1), [("y", g, k, 0), ("x", g, k, 1)], outs[1 + 1]
             todo["Q", g, k] = (4, g, 2), base, outs[1]
             every += [name for out in outs for name, _, _ in out]
-        for p in range(pieces):
-            todo["G", g, p] = (5, g, p), every, []
+        todo["N", g] = (5, g, 0), every, []
+        if g % pair == pair - 1:
+            for p in range(pieces):
+                todo["G", g // pair, p] = (6, g, p), [("N", i) for i in range(g + 1)], []
     clock, order, arrived = 0.0, [], {}
     free = dict.fromkeys("xyz", 0.0)
     while todo:
@@ -442,31 +444,66 @@
         arrive(("x", g, k, 1), piece(g, (1, 0, k), 1))
         pass_on(("fy", g, k), g, (1, 0, k), 1, y_dev)
 
-    def score_group(g, p):
-        r0, count = g * 4 * gr, 4 * gr
-        if p == 0:
-            arrive(("fx", g, 0), newref.at[pl.ds(r0, 2 * gr)])
-
-            def squares(i):
-                square_sums(newref, pl.multiple_of(r0 + i * 32, 32), 32, 1.0 / width)
-
-            each(count // 32, squares)
+    def new_norms(g):
+        arrive(("fx", g, 0), newref.at[pl.ds(g * 4 * gr, 2 * gr)])
+
+        def squares(i):
+            square_sums(newref, pl.multiple_of(g * 4 * gr + i * 64, 64), 64, 1.0 / width)
+
+        each(4 * gr // 64, squares)
+
+    pair = PAIR if groups % PAIR == 0 else 1
+    per_block = BLOCK // LANES
+
+    def likelihoods(c, h):
+        r0, count = c * pair * 4 * gr, pair * 4 * gr
+        chunks = [slice(r, min(r + ROWS, count)) for r in range(0, count, ROWS)]
 
         def body(i):
-            part = pl.ds(pl.multiple_of((p * per_piece + i) * LANES, LANES), LANES)
+            c0 = h * BLOCK + i * LANES
+            part = pl.ds(pl.multiple_of(c0, LANES), LANES)
             out = lax.dot_general(
                 newref[r0 : r0 + count, :], im[part, :], nt, preferred_element_type=F32
             )
-            cross[r0 : r0 + count, part] = out * width ** (-0.5)
-
-        each(per_piece, body)
-
-    per_piece = n // LANES // PIECES
+            slope, bend = coefficients(c0, LANES)
+            slope = [x * width ** (-0.5) for x in slope]
+            to = pl.ds(pl.multiple_of(i * LANES, 128), LANES)
+            highs, totals = [], []
+            for t in range(LANES // 128):
+                sc = []
+                for rr in chunks:
+                    nrm = fold(norms[r0 + rr.start : r0 + rr.stop, :])
+                    sc.append(
+                        slope[t][None] * fold(out[rr, t * 128 : (t + 1) * 128])
+                        - bend[t][None] * nrm
+                    )
+                high = functools.reduce(jnp.maximum, [jnp.max(x, axis=0) for x in sc])
+                high = jnp.max(high, axis=0, keepdims=True)
+                total = functools.reduce(
+                    jnp.add, [jnp.sum(jnp.exp2(x - spread8(high)[None]), axis=0) for x in sc]
+                )
+                highs.append(high)
+                totals.append(jnp.sum(total, axis=0, keepdims=True))
+            high = jnp.concatenate(highs, axis=1)
+            total = jnp.concatenate(totals, axis=1)
+            if c > 0:
+                before, sum_before = stat_snd[ITERS + 1, h, 0:1, to], stat_snd[ITERS + 1, h, 1:2, to]
+                top = jnp.maximum(before, high)
+                total = sum_before * jnp.exp2(before - top) + total * jnp.exp2(high - top)
+                high = top
+            stat_snd[ITERS + 1, h, 0:1, to] = high
+            stat_snd[ITERS + 1, h, 1:2, to] = total
+
+        each(per_block, body)
+        if c == groups // pair - 1:
+            for k in range(1, n_ref):
+                stat_copy(ITERS + 1, h, k).start()
+
     steps = {
         "S1": send1, "S2": send2, "Z": send3, "A": finish, "P": spread_first,
-        "Q": spread_second, "F": forward, "G": score_group,
+        "Q": spread_second, "F": forward, "N": new_norms, "G": likelihoods,
     }
-    order = plan(groups, nz, rg * width, PIECES)
+    order = plan(groups, nz, rg * width, blocks, pair)
     first = [name for name in order if name[0] == "S1" and name[1] < 2]
     rest = [name for name in order if name not in first]
 
@@ -489,7 +526,6 @@
             high * math.log(2.0) + jnp.log(total) - math.log(rows * n_ref)
         )
 
-    each(blocks, lambda h: local_stats(ITERS + 1, h, False))
     each(blocks, final_likelihood)
     def all_sent(like, sem):
         pltpu.make_async_copy(like, like, sem).wait()
@@ -500,6 +536,15 @@
         all_sent(like, ssem.at[kind])
     all_sent(newref.at[pl.ds(0, 2 * qr)], ssem.at[4])
     all_sent(newref.at[pl.ds(0, qr)], ssem.at[5])
+
+
+def put_out(new_vmem, contrast_vmem, loglik_vmem, new_hbm, contrast_hbm, loglik_hbm, sem):
+    pairs = ((new_vmem, new_hbm), (contrast_vmem, contrast_hbm), (loglik_vmem, loglik_hbm))
+    copies = [pltpu.make_async_copy(a, b, sem.at[i]) for i, (a, b) in enumerate(pairs)]
+    for copy in copies:
+        copy.start()
+    for copy in copies:
+        copy.wait()
 
 
 def per_device(nz, n_ref, images, references, initial_contrast):
@@ -563,6 +608,18 @@
             flops=flops, bytes_accessed=2 * n * width, transcendentals=0
         ),
     )(images, references, initial_contrast[None, :])
+    anywhere = pl.BlockSpec(memory_space=pl.ANY)
+    new_references, contrast, loglik = pl.pallas_call(
+        put_out,
+        out_shape=(
+            jax.ShapeDtypeStruct((rows, width), BF16),
+            jax.ShapeDtypeStruct((1, n), F32),
+            jax.ShapeDtypeStruct((1, n), F32),
+        ),
+        in_specs=[pl.BlockSpec(memory_space=pltpu.VMEM)] * 3,
+        out_specs=(anywhere,) * 3,
+        scratch_shapes=[pltpu.SemaphoreType.DMA((3,))],
+    )(*(pltpu.with_memory_space_constraint(v, pltpu.VMEM) for v in (new_references, contrast, loglik)))
     return (new_references, contrast[0], loglik[0])
 
 

time: 70.9 us -> 67.1 us (0.946)
  local copies, waits for them, and re-layouts: 2.51 us -> 0 us
  Pallas kernels: 67.6 us -> 66.3 us
    pallas_call x1, Pallas kernels: 67.6 us -> 65 us  [per_device(): pl.pallas_call(functools.partial(kernel, nz, n_ref), out_shape=(pltpu.VME...]
    unnamed x3 -> x0, local copies, waits for them, and re-layouts: 2.51 us -> none
    pallas_call x0 -> x1, Pallas kernels: none -> 1.35 us  [per_device(): pl.pallas_call(put_out, out_shape=(jax.ShapeDtypeStruct((rows, width), BF...]
where the time goes in v4:
time: 67.1 us; the launch traced here: 66.9 us
  Pallas kernels  66.3 us (99%)
    pallas_call x1, Pallas kernels, per_device(): pl.pallas_call(functools.partial(kernel, nz, n_ref), out_shape=(pltpu.VME...  65 us
    pallas_call x1, Pallas kernels, per_device(): pl.pallas_call(put_out, out_shape=(jax.ShapeDtypeStruct((rows, width), BF...  1.35 us

profile of v4, /device:TPU:0, one launch (start us, length us, event | category | flops | bytes accessed | tf_op | source)
XLA Modules:
  0.0 66.9 jit_solution(3508391287853593926)
XLA Ops:
  0.6 65.0 %shard_map.58 = (bf16[512,2048]{1,0:T(8,128)(2,1)S(1)}, f32[1,1024]{1,0:T(1,128)S(1)}, f32[1,1024]{1,0:T(1,128)S(1)}) custom-call(bf16[1024,2048]{1,0:T(8,128)(2,1)} %im_hbm.1, bf16[512,2048]{1,0:T(8,128)(2,1)} %ref_hbm.1, f32[1,1024]{1,0:T(1,128)} %bitcast.3), custom_call_target="tpu_custom_call" | custom-call | flops 6442450944 | bytes 4194304 | tf_op jit(solution)/shard_map/pallas_call | solution.py:561
  65.6 1.4 %shard_map.59 = (bf16[512,2048]{1,0:T(8,128)(2,1)}, f32[1,1024]{1,0:T(1,128)}, f32[1,1024]{1,0:T(1,128)}) custom-call(bf16[512,2048]{1,0:T(8,128)(2,1)S(1)} %get-tuple-element.9.new_vmem, f32[1,1024]{1,0:T(1,128)S(1)} %get-tuple-element.10.contrast_vmem, f32[1,1024]{1,0:T(1,128)S(1)} %get-tuple-element.11.loglik_vmem), custom_call_target="tpu_custom_call" | custom-call | tf_op jit(solution)/shard_map/pallas_call | solution.py:612

commit v5 on v4

--- a/solution.py
+++ b/solution.py
@@ -24,31 +24,57 @@
 F32 = jnp.float32
 BF16 = jnp.bfloat16
 
-RATE = 46.5e3
-HOP = 2.1
-FAR = 0.6
-BACKLOG = 0.5
-STEP = 0.12
-SCORE = 0.6
+RATE = 48e3
+HOP = 3.0
+FAR = 0.3
+BACKLOG = 0.7
+EAGER = 1
+DIRECT = 1
+COST = {"W": 1.27, "S2": 0.04, "Z": 0.06, "A": 0.11, "N": 0.2, "G": 1.1}
 PAIR = 2
+
+
+def low(k):
+    return k & -k
 
 
 def plan(groups, nz, block, pieces, pair):
     unit = block / RATE
     zs = range(1, nz)
-    todo = {}
+    bits = [1 << j for j in range(nz.bit_length() - 1)]
+    todo = {("W", s): ((-1, s, 0), [("W", s - 1)] if s else [], []) for s in range(4)}
     for g in range(groups):
         for s in (0, 1):
             for j in (0, 1):
-                todo["S1", g, s, j] = (2, g, 0), (), [(("s1", g, s, j), "xy"[s], unit * nz)]
+                todo["S1", g, s, j] = (
+                    (-2 if g < EAGER else 2, g, j), [("W", s)],
+                    [(("s1", g, s, j), "xy"[s], unit * nz)],
+                )
             todo["S2", g, s] = (
-                (1, g, 0), [("s1", g, s, 0)], [(("s2", g, s), "yx"[s], unit * nz)]
+                (1, g, 0), [("s1", g, s, 0), ("W", 3)], [(("s2", g, s), "yx"[s], unit * nz)]
             )
         met = [("s1", g, s, 1) for s in (0, 1)] + [("s2", g, s) for s in (0, 1)]
         met_z = [("z", g, k) for k in zs]
-        weight = {k: 2 * unit * (1.0 if k == 1 else 1.5) for k in zs}
-        todo["Z", g] = (0, g, 0), met, [(("z", g, k), "z", weight[k]) for k in zs]
-        todo["A", g] = (0, g, 0), met + met_z, [(("az", g, k), "z", weight[k]) for k in zs]
+        if g < DIRECT:
+            weight = {k: 2 * unit * (1.0 if k == 1 else 1.5) for k in zs}
+            todo["Z", g, 0] = (0, g, 0), met, [(("z", g, k), "z", weight[k]) for k in zs]
+            az = zs
+        else:
+            weight = dict.fromkeys(zs, 2 * unit)
+            for bit in bits:
+                inner = [("z", g, k) for k in zs if low(k) < bit and k > low(k)]
+                todo["Z", g, bit] = (
+                    (0, g, bit), met + inner,
+                    [(("z", g, k), "z", weight[k]) for k in zs if low(k) == bit][::-1],
+                )
+            az = bits[::-1]
+            for k in zs:
+                if low(k) > 1:
+                    todo["T", g, k] = (
+                        (0, g, 0), [("az", g, k)],
+                        [(("az", g, k + b), "z", weight[k]) for b in az if b < low(k)],
+                    )
+        todo["A", g] = (0, g, 0), met + met_z, [(("az", g, k), "z", weight[k]) for k in az]
         every = []
         for k in range(nz):
             base = [("az", g, k)] if k else [("A", g)]
@@ -70,18 +96,21 @@
         for name, (rank, waits, out) in todo.items():
             if all(wait in arrived for wait in waits):
                 start = max([arrived[wait] for wait in waits], default=0.0)
-                start = max([start, clock] + [free[link] - BACKLOG for _, link, _ in out])
+                start = max(start, clock)
+                if rank[0] > -2:
+                    start = max([start] + [free[link] - BACKLOG for _, link, _ in out])
                 if best is None or (start, rank, name) < best:
                     best = (start, rank, name)
         start, _, name = best
         out = todo.pop(name)[2]
-        clock = start + (SCORE if name[0] == "G" else STEP)
+        clock = start + COST.get(name[0], 0.02)
         arrived[name] = clock
         for message, link, length in out:
             free[link] = max(free[link], clock) + length
             arrived[message] = free[link] + HOP
-            if link == "z" and message[2] > 1:
-                arrived[message] += FAR
+            if link == "z":
+                far = message[2] if message[1] < DIRECT else low(message[2])
+                arrived[message] += FAR if far > 1 else 0.0
         order.append(name)
     return order
 
@@ -95,7 +124,7 @@
     n, width = im.shape
     rows = refs.shape[0]
     groups = own.shape[0]
-    rg = own.shape[1]
+    rg = own.shape[2]
     gr = nz * rg
     qr = groups * gr
     half = width // 2
@@ -354,7 +383,8 @@
     hop_dev = (x_dev, y_dev)
     landed = set()
     kinds = {"s1": 0, "s2": 1, "z": 2, "az": 3, "y": 4, "x": 4, "fx": 5, "fy": 5}
-    per_group = 2 + 1 + (nz - 1) + 2 * nz + 2
+    per_group = 4 * nz + 2
+    bits = [1 << j for j in range(nz.bit_length() - 1)]
 
     def slot_of(name):
         kind, g = name[:2]
@@ -363,13 +393,13 @@
         elif kind in ("s1", "s2"):
             at = 2
         elif kind == "z":
-            at = 3
+            at = 2 + name[2]
         elif kind == "az":
-            at = 3 + name[2]
+            at = 1 + nz + name[2]
         elif kind in ("x", "y") and name[3] == (kind == "x"):
-            at = 3 + nz + 2 * name[2] + (kind == "x")
+            at = 1 + 2 * nz + 2 * name[2] + (kind == "x")
         else:
-            at = 3 + 3 * nz
+            at = 1 + 4 * nz
         return g * per_group + at
 
     def put(name, src, dst, dev):
@@ -391,33 +421,52 @@
         snd2[s, part, :] = (acc[s * 2, part, :] + rcv1[s * 2, part, :].astype(F32)).astype(BF16)
         put(("s2", g, s), snd2.at[s, part], rcv2.at[s, part], hop_dev[1 - s])
 
-    def send3(g):
+    def send3(g, bit):
         part = pl.ds(g * gr, gr)
-        arrive(("s2", g, 0), rcv1.at[:, part])
-        for s in (0, 1):
-            total = (
-                acc[s * 2 + 1, part, :]
-                + rcv1[s * 2 + 1, part, :].astype(F32)
-                + rcv2[s, part, :].astype(F32)
-            )
-            cols = slice(s * half, (s + 1) * half)
-            own[g, :, cols] = total[0:rg]
-            for k in range(1, nz):
-                snd3[g, k - 1, :, cols] = total[k * rg : (k + 1) * rg].astype(BF16)
-        for k in range(1, nz):
-            put(("z", g, k), snd3.at[g, k - 1], rcv3.at[g, k - 1], z_dev[k])
+        if bit < 2:
+            arrive(("s2", g, 0), rcv1.at[:, part])
+            for s in (0, 1):
+                total = (
+                    acc[s * 2 + 1, part, :]
+                    + rcv1[s * 2 + 1, part, :].astype(F32)
+                    + rcv2[s, part, :].astype(F32)
+                )
+                cols = slice(s * half, (s + 1) * half)
+                for k in range(nz):
+                    block = total[k * rg : (k + 1) * rg]
+                    if k and (bit == 0 or low(k) == 1):
+                        snd3[g, k - 1, :, cols] = block.astype(BF16)
+                    else:
+                        own[g, k, :, cols] = block
+        for k in range(nz - 1, 0, -1):
+            if bit and low(k) != bit:
+                continue
+            if bit > 1:
+                total = own[g, k]
+                for c in bits:
+                    if c < bit:
+                        arrive(("z", g, k + c), rcv3.at[g, 0])
+                        total = total + rcv3[g, k + c - 1].astype(F32)
+                snd3[g, k - 1] = total.astype(BF16)
+            put(("z", g, k), snd3.at[g, k - 1], rcv3.at[g, k - 1], z_dev[bit or k])
 
     def finish(g):
-        total = own[g]
-        if nz > 1:
-            arrive(("z", g, 1), rcv3.at[g])
-        for k in range(1, nz):
+        total = own[g, 0]
+        for k in range(1, nz) if g < DIRECT else bits:
+            arrive(("z", g, k), rcv3.at[g, 0])
             total = total + rcv3[g, k - 1].astype(F32)
         square = jnp.sum(total * total, axis=1, keepdims=True)
         mine = pl.ds(row0(g, (0, 0, 0)), rg)
         newref[mine, :] = (total * lax.rsqrt(square / width + epsilon)).astype(BF16)
-        for k in range(1, nz):
+        for k in range(1, nz) if g < DIRECT else bits[::-1]:
             put(("az", g, k), newref.at[mine], newref.at[mine], z_dev[k])
+
+    def relay(g, k):
+        part = newref.at[pl.ds(row0(g, (0, 0, k)), rg)]
+        arrive(("az", g, k), part)
+        for bit in bits[::-1]:
+            if bit < low(k):
+                put(("az", g, k + bit), part, part, z_dev[bit])
 
     def piece(g, where, side):
         return newref.at[pl.ds(row0(g, where), rg), pl.ds(side * half, half)]
@@ -500,23 +549,18 @@
                 stat_copy(ITERS + 1, h, k).start()
 
     steps = {
-        "S1": send1, "S2": send2, "Z": send3, "A": finish, "P": spread_first,
+        "S1": send1, "S2": send2, "Z": send3, "A": finish, "T": relay, "P": spread_first,
         "Q": spread_second, "F": forward, "N": new_norms, "G": likelihoods,
     }
     order = plan(groups, nz, rg * width, blocks, pair)
-    first = [name for name in order if name[0] == "S1" and name[1] < 2]
-    rest = [name for name in order if name not in first]
-
-    weighted([(0, 2 * qr)], 0, to_send(0, False))
-    for name in first:
-        if name[2] == 0:
-            send1(*name[1:])
-    weighted([(qr, 2 * qr)], half, to_send(1, True))
-    for name in first:
-        if name[2] == 1:
-            send1(*name[1:])
-    weighted([(2 * qr, 2 * qr)], 0, to_keep(0))
-    weighted([(0, qr), (3 * qr, qr)], half, to_keep(1))
+    sums = (
+        functools.partial(weighted, [(0, 2 * qr)], 0, to_send(0, False)),
+        functools.partial(weighted, [(qr, 2 * qr)], half, to_send(1, True)),
+        functools.partial(weighted, [(2 * qr, 2 * qr)], 0, to_keep(0)),
+        functools.partial(weighted, [(0, qr), (3 * qr, qr)], half, to_keep(1)),
+    )
+    steps["W"] = lambda part: sums[part]()
+    rest = order
     for name in rest:
         steps[name[0]](*name[1:])
 
@@ -556,7 +600,7 @@
     steps = ITERS + 2
     peers = max(n_ref - 1, 1)
     stat_copies = steps * (n // BLOCK) * peers
-    arrivals = groups * (2 + 1 + (nz - 1) + 2 * nz + 2)
+    arrivals = groups * (4 * nz + 2)
     flops = 6 * n * width * rows
     new_references, contrast, loglik = pl.pallas_call(
         functools.partial(kernel, nz, n_ref),
@@ -588,7 +632,7 @@
             pltpu.VMEM((2, qr, half), BF16),
             pltpu.VMEM((groups, max(nz - 1, 1), rg, width), BF16),
             pltpu.VMEM((groups, max(nz - 1, 1), rg, width), BF16),
-            pltpu.VMEM((groups, rg, width), F32),
+            pltpu.VMEM((groups, nz, rg, width), F32),
             pltpu.VMEM((steps, n // BLOCK, 4, BLOCK), F32),
             pltpu.VMEM((stat_copies, 4, BLOCK), F32),
             pltpu.VMEM((8, n), F32),

time: 67.1 us -> 65.1 us (0.970)
  Pallas kernels: 66.3 us -> 64.3 us
    pallas_call x1, Pallas kernels: 65 us -> 62.9 us  [per_device(): pl.pallas_call(functools.partial(kernel, nz, n_ref), out_shape=(pltpu.VME...]
where the time goes in v5:
time: 65.1 us; the launch traced here: 64.9 us
  Pallas kernels  64.3 us (99%)
    pallas_call x1, Pallas kernels, per_device(): pl.pallas_call(functools.partial(kernel, nz, n_ref), out_shape=(pltpu.VME...  62.9 us
    pallas_call x1, Pallas kernels, per_device(): pl.pallas_call(put_out, out_shape=(jax.ShapeDtypeStruct((rows, width), BF...  1.35 us

profile of v5, /device:TPU:0, one launch (start us, length us, event | category | flops | bytes accessed | tf_op | source)
XLA Modules:
  0.0 64.9 jit_solution(11529739908671418689)
XLA Ops:
  0.6 62.9 %shard_map.58 = (bf16[512,2048]{1,0:T(8,128)(2,1)S(1)}, f32[1,1024]{1,0:T(1,128)S(1)}, f32[1,1024]{1,0:T(1,128)S(1)}) custom-call(bf16[1024,2048]{1,0:T(8,128)(2,1)} %im_hbm.1, bf16[512,2048]{1,0:T(8,128)(2,1)} %ref_hbm.1, f32[1,1024]{1,0:T(1,128)} %bitcast.3), custom_call_target="tpu_custom_call" | custom-call | flops 6442450944 | bytes 4194304 | tf_op jit(solution)/shard_map/pallas_call | solution.py:605
  63.6 1.4 %shard_map.59 = (bf16[512,2048]{1,0:T(8,128)(2,1)}, f32[1,1024]{1,0:T(1,128)}, f32[1,1024]{1,0:T(1,128)}) custom-call(bf16[512,2048]{1,0:T(8,128)(2,1)S(1)} %get-tuple-element.9.new_vmem, f32[1,1024]{1,0:T(1,128)S(1)} %get-tuple-element.10.contrast_vmem, f32[1,1024]{1,0:T(1,128)S(1)} %get-tuple-element.11.loglik_vmem), custom_call_target="tpu_custom_call" | custom-call | tf_op jit(solution)/shard_map/pallas_call | solution.py:656

commit v6 on v5

--- a/solution.py
+++ b/solution.py
@@ -16,6 +16,7 @@
 
 MESH = pl.DeviceIdType.MESH
 LANES = 256
+AHEAD = 2
 BLOCK = 512
 TILES = BLOCK // 128
 ROWS = 128
@@ -24,12 +25,13 @@
 F32 = jnp.float32
 BF16 = jnp.bfloat16
 
-RATE = 48e3
-HOP = 3.0
-FAR = 0.3
-BACKLOG = 0.7
+RATE = 46.5e3
+HOP = 2.7
+FAR = 0.0
+BACKLOG = 0.9
 EAGER = 1
 DIRECT = 1
+RANK = {"S1": 2, "S2": 1, "P": 4, "F": 4, "Q": 4}
 COST = {"W": 1.27, "S2": 0.04, "Z": 0.06, "A": 0.11, "N": 0.2, "G": 1.1}
 PAIR = 2
 
@@ -47,11 +49,11 @@
         for s in (0, 1):
             for j in (0, 1):
                 todo["S1", g, s, j] = (
-                    (-2 if g < EAGER else 2, g, j), [("W", s)],
+                    (-2 if g < EAGER else RANK["S1"], g, j), [("W", s)],
                     [(("s1", g, s, j), "xy"[s], unit * nz)],
                 )
             todo["S2", g, s] = (
-                (1, g, 0), [("s1", g, s, 0), ("W", 3)], [(("s2", g, s), "yx"[s], unit * nz)]
+                (RANK["S2"], g, 0), [("s1", g, s, 0), ("W", 3)], [(("s2", g, s), "yx"[s], unit * nz)]
             )
         met = [("s1", g, s, 1) for s in (0, 1)] + [("s2", g, s) for s in (0, 1)]
         met_z = [("z", g, k) for k in zs]
@@ -81,9 +83,9 @@
             outs = [[(("y", g, k, 0), "y", unit), (("x", g, k, 1), "x", unit)]]
             outs.append([(("y", g, k, 1), "y", unit), (("x", g, k, 0), "x", unit)])
             outs.append([(("fx", g, k), "x", unit), (("fy", g, k), "y", unit)])
-            todo["P", g, k] = (4, g, 0), base, outs[0]
-            todo["F", g, k] = (4, g, 1), [("y", g, k, 0), ("x", g, k, 1)], outs[1 + 1]
-            todo["Q", g, k] = (4, g, 2), base, outs[1]
+            todo["P", g, k] = (RANK["P"], g, 0), base, outs[0]
+            todo["F", g, k] = (RANK["F"], g, 1), [("y", g, k, 0), ("x", g, k, 1)], outs[1 + 1]
+            todo["Q", g, k] = (RANK["Q"], g, 2), base, outs[1]
             every += [name for out in outs for name, _, _ in out]
         todo["N", g] = (5, g, 0), every, []
         if g % pair == pair - 1:
@@ -162,9 +164,13 @@
         copy = pltpu.make_async_copy(ref_hbm.at[part], refs.at[part], ref_sem.at[s])
         copy.start()
         ref_copies.append(copy)
-    for b in range(n // LANES):
-        part = pl.ds(b * LANES, LANES)
-        pltpu.make_async_copy(im_hbm.at[part], im.at[part], im_sem.at[b]).start()
+    def load_images(b):
+        part = pl.ds(pl.multiple_of(b * LANES, LANES), LANES)
+        return pltpu.make_async_copy(im_hbm.at[part], im.at[part], im_sem.at[b])
+
+    ahead = min(AHEAD, n // LANES)
+    for b in range(ahead):
+        load_images(b).start()
     prior_copy = pltpu.make_async_copy(prior_hbm, vecs.at[3:4, :], prior_sem)
     prior_copy.start()
 
@@ -175,10 +181,11 @@
         total = jnp.sum(block * block, axis=1, keepdims=True) * scale
         norms[pl.ds(r0, count), :] = jnp.broadcast_to(total, (count, 128))
 
-    for s, copy in enumerate(ref_copies):
+    for copy in ref_copies:
         copy.wait()
-        for r0 in range(s * per_ref, (s + 1) * per_ref, 32):
-            square_sums(refs, r0, 32, 1.0)
+    for b in range(ahead, n // LANES):
+        load_images(b).start()
+    per_block = rows // (n // LANES)
 
     nt = (((1,), (1,)), ((), ()))
     nn = (((1,), (0,)), ((), ()))
@@ -285,7 +292,7 @@
             device_id=r_dev[k], device_id_type=MESH,
         )
 
-    def local_stats(it, h, full):
+    def local_stats(it, h, full, first=False):
         c0 = h * BLOCK
         high = scores(c0)
         sums = sums_of(c0, high, full)
@@ -294,6 +301,12 @@
             stat_snd[it, h, 0:1, at] = high[t]
             for j in range(len(sums) // TILES):
                 stat_snd[it, h, j + 1 : j + 2, at] = sums[j * TILES + t]
+        if first:
+
+            @pl.when(h == 0)
+            def _():
+                pl.semaphore_wait(barrier, len(peers))
+
         for k in range(1, n_ref):
             stat_copy(it, h, k).start()
 
@@ -325,7 +338,9 @@
 
     def first_cross(b):
         part = pl.ds(pl.multiple_of(b * LANES, LANES), LANES)
-        pltpu.make_async_copy(im_hbm.at[part], im.at[part], im_sem.at[b]).wait()
+        load_images(b).wait()
+        for r in range(0, per_block, 32):
+            square_sums(refs, pl.multiple_of(b * per_block + r, 32), 32, 1.0)
         cross[:, part] = lax.dot_general(
             refs[...], im[part, :], nt, preferred_element_type=F32
         )
@@ -347,8 +362,7 @@
         weigh(h * BLOCK)
 
     each(n // LANES, first_cross)
-    pl.semaphore_wait(barrier, len(peers))
-    each(blocks, lambda h: local_stats(0, h, True))
+    each(blocks, lambda h: local_stats(0, h, True, True))
     each(ITERS * blocks, refit)
     each(blocks, settle)
     contrast_ref[...] = vecs[0:1, :]
@@ -383,7 +397,7 @@
     hop_dev = (x_dev, y_dev)
     landed = set()
     kinds = {"s1": 0, "s2": 1, "z": 2, "az": 3, "y": 4, "x": 4, "fx": 5, "fy": 5}
-    per_group = 4 * nz + 2
+    per_group = 3 * nz + 2
     bits = [1 << j for j in range(nz.bit_length() - 1)]
 
     def slot_of(name):
@@ -397,9 +411,9 @@
         elif kind == "az":
             at = 1 + nz + name[2]
         elif kind in ("x", "y") and name[3] == (kind == "x"):
-            at = 1 + 2 * nz + 2 * name[2] + (kind == "x")
+            at = 1 + 2 * nz + name[2]
         else:
-            at = 1 + 4 * nz
+            at = 1 + 3 * nz
         return g * per_group + at
 
     def put(name, src, dst, dev):
@@ -488,9 +502,8 @@
         pass_on(("x", g, k, 0), g, (0, 0, k), 0, x_dev)
 
     def forward(g, k):
-        arrive(("y", g, k, 0), piece(g, (0, 1, k), 0))
+        arrive(("y", g, k, 0), newref.at[pl.ds(row0(g, (0, 1, k)), rg)])
         pass_on(("fx", g, k), g, (0, 1, k), 0, x_dev)
-        arrive(("x", g, k, 1), piece(g, (1, 0, k), 1))
         pass_on(("fy", g, k), g, (1, 0, k), 1, y_dev)
 
     def new_norms(g):
@@ -502,7 +515,7 @@
         each(4 * gr // 64, squares)
 
     pair = PAIR if groups % PAIR == 0 else 1
-    per_block = BLOCK // LANES
+    per_slot = BLOCK // LANES
 
     def likelihoods(c, h):
         r0, count = c * pair * 4 * gr, pair * 4 * gr
@@ -543,7 +556,8 @@
             stat_snd[ITERS + 1, h, 0:1, to] = high
             stat_snd[ITERS + 1, h, 1:2, to] = total
 
-        each(per_block, body)
+        for i in range(per_slot):
+            body(i)
         if c == groups // pair - 1:
             for k in range(1, n_ref):
                 stat_copy(ITERS + 1, h, k).start()
@@ -600,7 +614,7 @@
     steps = ITERS + 2
     peers = max(n_ref - 1, 1)
     stat_copies = steps * (n // BLOCK) * peers
-    arrivals = groups * (4 * nz + 2)
+    arrivals = groups * (3 * nz + 2)
     flops = 6 * n * width * rows
     new_references, contrast, loglik = pl.pallas_call(
         functools.partial(kernel, nz, n_ref),

time: 65.1 us -> 63.2 us (0.971)
  Pallas kernels: 64.3 us -> 62.4 us
    pallas_call x1, Pallas kernels: 62.9 us -> 61.1 us  [per_device(): pl.pallas_call(functools.partial(kernel, nz, n_ref), out_shape=(pltpu.VME...]
where the time goes in v6:
time: 63.2 us; the launch traced here: 63.1 us
  Pallas kernels  62.4 us (99%)
  between operations  0.64 us (1%)
    pallas_call x1, Pallas kernels, per_device(): pl.pallas_call(functools.partial(kernel, nz, n_ref), out_shape=(pltpu.VME...  61.1 us
    pallas_call x1, Pallas kernels, per_device(): pl.pallas_call(put_out, out_shape=(jax.ShapeDtypeStruct((rows, width), BF...  1.35 us

profile of v6, /device:TPU:0, one launch (start us, length us, event | category | flops | bytes accessed | tf_op | source)
XLA Modules:
  0.0 63.1 jit_solution(6433568733427475956)
XLA Ops:
  0.6 61.1 %shard_map.58 = (bf16[512,2048]{1,0:T(8,128)(2,1)S(1)}, f32[1,1024]{1,0:T(1,128)S(1)}, f32[1,1024]{1,0:T(1,128)S(1)}) custom-call(bf16[1024,2048]{1,0:T(8,128)(2,1)} %im_hbm.1, bf16[512,2048]{1,0:T(8,128)(2,1)} %ref_hbm.1, f32[1,1024]{1,0:T(1,128)} %bitcast.3), custom_call_target="tpu_custom_call" | custom-call | flops 6442450944 | bytes 4194304 | tf_op jit(solution)/shard_map/pallas_call | solution.py:619
  61.7 1.4 %shard_map.59 = (bf16[512,2048]{1,0:T(8,128)(2,1)}, f32[1,1024]{1,0:T(1,128)}, f32[1,1024]{1,0:T(1,128)}) custom-call(bf16[512,2048]{1,0:T(8,128)(2,1)S(1)} %get-tuple-element.9.new_vmem, f32[1,1024]{1,0:T(1,128)S(1)} %get-tuple-element.10.contrast_vmem, f32[1,1024]{1,0:T(1,128)S(1)} %get-tuple-element.11.loglik_vmem), custom_call_target="tpu_custom_call" | custom-call | tf_op jit(solution)/shard_map/pallas_call | solution.py:670

commit v7 on v6

--- a/solution.py
+++ b/solution.py
@@ -25,14 +25,14 @@
 F32 = jnp.float32
 BF16 = jnp.bfloat16
 
-RATE = 46.5e3
+RATE = 48e3
 HOP = 2.7
 FAR = 0.0
 BACKLOG = 0.9
 EAGER = 1
 DIRECT = 1
 RANK = {"S1": 2, "S2": 1, "P": 4, "F": 4, "Q": 4}
-COST = {"W": 1.27, "S2": 0.04, "Z": 0.06, "A": 0.11, "N": 0.2, "G": 1.1}
+COST = {"W": 1.1, "S2": 0.04, "Z": 0.06, "A": 0.11, "N": 0.2, "G": 1.1}
 PAIR = 2
 
 
@@ -377,7 +377,8 @@
             store(pl.ds(col, LANES), out[:qr], out[qr:])
             return carry
 
-        lax.fori_loop(0, half // LANES, body, 0)
+        for b in range(half // LANES):
+            body(b, 0)
 
     def to_send(stream, first_is_far):
         def store(cols, lo, hi):
@@ -509,10 +510,12 @@
     def new_norms(g):
         arrive(("fx", g, 0), newref.at[pl.ds(g * 4 * gr, 2 * gr)])
 
+        step = math.gcd(4 * gr, 128)
+
         def squares(i):
-            square_sums(newref, pl.multiple_of(g * 4 * gr + i * 64, 64), 64, 1.0 / width)
-
-        each(4 * gr // 64, squares)
+            square_sums(newref, pl.multiple_of(g * 4 * gr + i * step, 8), step, 1.0 / width)
+
+        each(4 * gr // step, squares)
 
     pair = PAIR if groups % PAIR == 0 else 1
     per_slot = BLOCK // LANES

time: 63.2 us -> 61.7 us (0.976)
  Pallas kernels: 62.4 us -> 60.9 us
    pallas_call x1, Pallas kernels: 61.1 us -> 59.5 us  [per_device(): pl.pallas_call(functools.partial(kernel, nz, n_ref), out_shape=(pltpu.VME...]
where the time goes in v7:
time: 61.7 us; the launch traced here: 61.5 us
  Pallas kernels  60.9 us (99%)
  between operations  0.64 us (1%)
    pallas_call x1, Pallas kernels, per_device(): pl.pallas_call(functools.partial(kernel, nz, n_ref), out_shape=(pltpu.VME...  59.5 us
    pallas_call x1, Pallas kernels, per_device(): pl.pallas_call(put_out, out_shape=(jax.ShapeDtypeStruct((rows, width), BF...  1.35 us

profile of v7, /device:TPU:0, one launch (start us, length us, event | category | flops | bytes accessed | tf_op | source)
XLA Modules:
  0.0 61.5 jit_solution(8991827610719573480)
XLA Ops:
  0.6 59.5 %shard_map.58 = (bf16[512,2048]{1,0:T(8,128)(2,1)S(1)}, f32[1,1024]{1,0:T(1,128)S(1)}, f32[1,1024]{1,0:T(1,128)S(1)}) custom-call(bf16[1024,2048]{1,0:T(8,128)(2,1)} %im_hbm.1, bf16[512,2048]{1,0:T(8,128)(2,1)} %ref_hbm.1, f32[1,1024]{1,0:T(1,128)} %bitcast.3), custom_call_target="tpu_custom_call" | custom-call | flops 6442450944 | bytes 4194304 | tf_op jit(solution)/shard_map/pallas_call | solution.py:622
  60.2 1.4 %shard_map.59 = (bf16[512,2048]{1,0:T(8,128)(2,1)}, f32[1,1024]{1,0:T(1,128)}, f32[1,1024]{1,0:T(1,128)}) custom-call(bf16[512,2048]{1,0:T(8,128)(2,1)S(1)} %get-tuple-element.9.new_vmem, f32[1,1024]{1,0:T(1,128)S(1)} %get-tuple-element.10.contrast_vmem, f32[1,1024]{1,0:T(1,128)S(1)} %get-tuple-element.11.loglik_vmem), custom_call_target="tpu_custom_call" | custom-call | tf_op jit(solution)/shard_map/pallas_call | solution.py:673

commit v8 on v7

--- a/solution.py
+++ b/solution.py
@@ -279,7 +279,8 @@
                     w[to, at] = jnp.concatenate(e, axis=0).astype(BF16)
             return carry
 
-        lax.fori_loop(0, groups, body, 0)
+        for g in range(groups):
+            body(g, 0)
 
     blocks = n // BLOCK
 
@@ -364,7 +365,8 @@
     each(n // LANES, first_cross)
     each(blocks, lambda h: local_stats(0, h, True, True))
     each(ITERS * blocks, refit)
-    each(blocks, settle)
+    for h in range(blocks):
+        settle(h)
     contrast_ref[...] = vecs[0:1, :]
 
     def weighted(r0s, c0, store):

time: 61.7 us -> 61.4 us (level)
  no operation moved by 1% of the time
where the time goes in v8:
time: 61.4 us; the launch traced here: 61.2 us
  Pallas kernels  60.6 us (99%)
  between operations  0.64 us (1%)
    pallas_call x1, Pallas kernels, per_device(): pl.pallas_call(functools.partial(kernel, nz, n_ref), out_shape=(pltpu.VME...  59.2 us
    pallas_call x1, Pallas kernels, per_device(): pl.pallas_call(put_out, out_shape=(jax.ShapeDtypeStruct((rows, width), BF...  1.35 us

profile of v8, /device:TPU:0, one launch (start us, length us, event | category | flops | bytes accessed | tf_op | source)
XLA Modules:
  0.0 61.2 jit_solution(15538281354936930940)
XLA Ops:
  0.6 59.2 %shard_map.58 = (bf16[512,2048]{1,0:T(8,128)(2,1)S(1)}, f32[1,1024]{1,0:T(1,128)S(1)}, f32[1,1024]{1,0:T(1,128)S(1)}) custom-call(bf16[1024,2048]{1,0:T(8,128)(2,1)} %im_hbm.1, bf16[512,2048]{1,0:T(8,128)(2,1)} %ref_hbm.1, f32[1,1024]{1,0:T(1,128)} %bitcast.3), custom_call_target="tpu_custom_call" | custom-call | flops 6442450944 | bytes 4194304 | tf_op jit(solution)/shard_map/pallas_call | solution.py:624
  59.9 1.4 %shard_map.59 = (bf16[512,2048]{1,0:T(8,128)(2,1)}, f32[1,1024]{1,0:T(1,128)}, f32[1,1024]{1,0:T(1,128)}) custom-call(bf16[512,2048]{1,0:T(8,128)(2,1)S(1)} %get-tuple-element.9.new_vmem, f32[1,1024]{1,0:T(1,128)S(1)} %get-tuple-element.10.contrast_vmem, f32[1,1024]{1,0:T(1,128)S(1)} %get-tuple-element.11.loglik_vmem), custom_call_target="tpu_custom_call" | custom-call | tf_op jit(solution)/shard_map/pallas_call | solution.py:675
